TPU v7x, 1024 devices: a whole 4x4x32 slice. The times are simulated.
1024 devices in a mesh: ctx: 64 (over x, z_lo), dp: 16 (over y, z_hi, core).
Axes of the slice: x: 4, y: 4, z: 32 (z_hi: 2, z_lo: 16; z = z_hi * 16 + z_lo), core: 2. Of those that a mesh axis runs over, the one named last changes fastest.
Arguments:
- xbc_raw: bfloat16 [16, 16384, 512], P('dp', 'ctx'), may hold values from -6 to 6
- conv_weight: float32 [4, 512], replicated, may hold values from -3 to 3
- conv_bias: float32 [512], replicated, may hold values from -3 to 3
- dt_raw: float32 [16, 16384, 4], P('dp', 'ctx'), may hold values from -1 to 10
- dt_bias: float32 [4], replicated, may hold values from -7.3 to -0.15
- a_log: float32 [4], replicated, may hold values from -3.5 to -2.5
- d_skip: float32 [4], replicated, may hold values from 0.5 to 1.5
- grad_out: bfloat16 [16, 16384, 256], P('dp', 'ctx'), may hold values from -6 to 6
Outputs:
- grad_xbc: bfloat16 [16, 16384, 512], P('dp', 'ctx')
- grad_dt: float32 [16, 16384, 4], P('dp', 'ctx')
- grad_conv_weight: float32 [4, 512], replicated
- grad_conv_bias: float32 [512], replicated
- grad_dt_bias: float32 [4], replicated
- grad_a_log: float32 [4], replicated
- grad_d_skip: float32 [4], replicated
All inputs are finite; a program needn't handle non-finite values.
Results may differ from a plain program's by a relative error of at most 0.0025.
The roundings to bfloat16 on the way count: a program that leaves them out, or rounds other values in their place, can miss the bound.
Values may be sent and summed in bfloat16 or wider, within the bound.
A program may use at most 32 MiB of HBM per device.

v0:
```python
import jax
import jax.numpy as jnp
from jax import lax
from jax.sharding import PartitionSpec as P

H = 4
P_SIZE = 64
N = 128
K = 4


highest = lax.Precision.HIGHEST


def prefix(part, axis, combine, identity, reverse):
    count = lax.axis_size(axis)
    place = lax.axis_index(axis)
    ahead = count - 1 - place if reverse else place
    gathered = jax.tree.map(lambda a: lax.all_gather(a, axis), part)
    state = jax.tree.map(lambda a, e: jnp.zeros_like(a) + jnp.asarray(e, a.dtype), part, identity)

    def one(turn, state):
        source = count - 1 - turn if reverse else turn
        return combine(
            state, jax.tree.map(lambda a: lax.dynamic_index_in_dim(a, source, 0, False), gathered)
        )

    return lax.fori_loop(0, ahead, one, state)


def from_behind(block, axis, distance):
    devices = range(lax.axis_size(axis))
    route = [(i - distance, i) for i in devices if i - distance in devices]
    return lax.ppermute(block, axis, route)


def chain_step(earlier, later):
    return (earlier[0] * later[0], later[1] + later[0][:, None, None] * earlier[1])


def carry_forward(block_decay, local_state):
    identity_pair = (jnp.ones_like(block_decay), jnp.zeros_like(local_state))
    result_pair = prefix((block_decay, local_state), "ctx", chain_step, identity_pair, False)
    carried = result_pair[1]
    return carried


def carry_back(block_decay, local_grad):
    identity_pair = (jnp.ones_like(block_decay), jnp.zeros_like(local_grad))
    result_pair = prefix((block_decay, local_grad), "ctx", chain_step, identity_pair, True)
    carried = result_pair[1]
    return carried


def reduce_grads(weight_grad, bias_grad, grad_bias, grad_alog, skip_grad):
    totals = lax.psum((weight_grad, bias_grad, grad_bias, grad_alog, skip_grad), ("ctx", "dp"))
    return totals


def on_device(xbc_raw, conv_weight, conv_bias, dt_raw, dt_bias, a_log, d_skip, grad_out):
    raw_rows = xbc_raw[0]
    tok_rows = raw_rows.shape[0]
    prior_rows = from_behind(raw_rows[tok_rows - K + 1 :], "ctx", 1)
    padded = jnp.concatenate([prior_rows, raw_rows], 0).astype(jnp.float32)
    pre_conv = conv_bias + sum(
        (conv_weight[tap_idx] * padded[tap_idx : tap_idx + tok_rows] for tap_idx in range(K))
    )
    xbc_low = lax.optimization_barrier(jax.nn.silu(pre_conv).astype(jnp.bfloat16))
    xbc = xbc_low.astype(jnp.float32)
    inner_width = H * P_SIZE
    values = xbc[:, :inner_width].reshape(tok_rows, H, P_SIZE)
    b_proj = xbc[:, inner_width : inner_width + N]
    c_proj = xbc[:, inner_width + N :]
    dt_pre = dt_raw[0] + dt_bias
    step_size = jax.nn.softplus(dt_pre)
    decay_rate = -jnp.exp(a_log)
    cum_log = jnp.cumsum(step_size * decay_rate, axis=0)
    cum_log_t = cum_log.T
    step_t = step_size.T
    causal = jnp.tril(jnp.ones((tok_rows, tok_rows), dtype=jnp.bool_))
    log_gaps = cum_log_t[:, :, None] - cum_log_t[:, None, :]
    within = jnp.where(causal, jnp.exp(jnp.where(causal, log_gaps, 0.0)), 0.0)
    gram_mat = jnp.dot(c_proj, b_proj.T, precision=highest)
    mixing = gram_mat[None] * within * step_t[:, None, :]
    tail_w = jnp.exp(cum_log_t[:, -1:] - cum_log_t) * step_t
    weighted = values * tail_w.T[:, :, None]
    local_state = jnp.einsum("shp,sn->hpn", weighted, b_proj, precision=highest)
    block_decay = jnp.exp(cum_log[-1])
    upstream = jnp.exp(cum_log)
    cotangent = grad_out[0].astype(jnp.float32).reshape(tok_rows, H, P_SIZE)
    scaled_cotan = cotangent * upstream[:, :, None]
    local_grad = jnp.einsum("thp,tn->hpn", scaled_cotan, c_proj, precision=highest)
    state_in = carry_forward(block_decay, local_state)
    grad_after = carry_back(block_decay, local_grad)
    dmix = jnp.where(causal, jnp.einsum("thp,shp->hts", cotangent, values, precision=highest), 0.0)
    state_back = jnp.einsum("hpn,sn->shp", grad_after, b_proj, precision=highest)
    grad_vals = jnp.einsum("hts,thp->shp", mixing, cotangent, precision=highest)
    grad_vals = grad_vals + d_skip[:, None] * cotangent + tail_w.T[:, :, None] * state_back
    skip_grad = jnp.sum(cotangent * values, axis=(0, 2))
    dgram = jnp.sum(dmix * within * step_t[:, None, :], axis=0)
    grad_c = jnp.einsum("thp,hpn->tn", scaled_cotan, state_in, precision=highest)
    grad_c = grad_c + jnp.dot(dgram, b_proj, precision=highest)
    grad_b = jnp.dot(dgram.T, c_proj, precision=highest)
    grad_b = grad_b + jnp.einsum("shp,hpn->sn", weighted, grad_after, precision=highest)
    grad_step = jnp.sum(dmix * gram_mat[None] * within, axis=1).T
    tail_grad = jnp.sum(values * state_back, axis=2)
    grad_step = grad_step + tail_grad * jnp.exp(cum_log[-1:] - cum_log)
    pair_terms = dmix * mixing
    grad_cum = jnp.sum(pair_terms, axis=2).T - jnp.sum(pair_terms, axis=1).T
    state_proj = jnp.einsum("tn,hpn->thp", c_proj, state_in, precision=highest)
    grad_cum = grad_cum + jnp.sum(scaled_cotan * state_proj, axis=2)
    tail_term = tail_grad * tail_w.T
    last_extra = jnp.sum(tail_term, axis=0) + block_decay * jnp.sum(
        grad_after * state_in, axis=(1, 2)
    )
    grad_cum = grad_cum - tail_term
    grad_cum = grad_cum.at[-1].add(last_extra)
    grad_log = jnp.flip(jnp.cumsum(jnp.flip(grad_cum, 0), axis=0), 0)
    grad_step = grad_step + decay_rate * grad_log
    grad_alog = jnp.sum(grad_log * step_size, axis=0) * decay_rate
    grad_pre = grad_step * jax.nn.sigmoid(dt_pre)
    grad_bias = jnp.sum(grad_pre, axis=0)
    grad_mid = jnp.concatenate([grad_vals.reshape(tok_rows, inner_width), grad_b, grad_c], 1)
    grad_low = lax.optimization_barrier(grad_mid.astype(jnp.bfloat16))
    grad_act = grad_low.astype(jnp.float32)
    sigmoid_z = jax.nn.sigmoid(pre_conv)
    grad_conv = grad_act * sigmoid_z * (1.0 + pre_conv * (1.0 - sigmoid_z))
    grad_padded = sum(
        (
            jnp.pad(conv_weight[tap_idx] * grad_conv, ((tap_idx, K - 1 - tap_idx), (0, 0)))
            for tap_idx in range(K)
        )
    )
    weight_grad = jnp.stack(
        [jnp.sum(grad_conv * padded[tap_idx : tap_idx + tok_rows], axis=0) for tap_idx in range(K)]
    )
    bias_grad = jnp.sum(grad_conv, axis=0)
    spill_rows = from_behind(grad_padded[: K - 1], "ctx", -1)
    grad_rows = grad_padded[K - 1 :]
    grad_rows = grad_rows.at[tok_rows - K + 1 :].add(spill_rows)
    grad_input = grad_rows.astype(jnp.bfloat16)[None]
    totals = reduce_grads(weight_grad, bias_grad, grad_bias, grad_alog, skip_grad)
    return (grad_input, grad_pre[None], totals[0], totals[1], totals[2], totals[3], totals[4])


def solution(mesh):
    in_specs = (
        P("dp", "ctx", None),
        P(),
        P(),
        P("dp", "ctx", None),
        P(),
        P(),
        P(),
        P("dp", "ctx", None),
    )
    out_specs = (P("dp", "ctx", None), P("dp", "ctx", None), P(), P(), P(), P(), P())
    return jax.shard_map(
        on_device, mesh=mesh, in_specs=in_specs, out_specs=out_specs, check_vma=False
    )
```

profile of v0, /device:TPU:1, one launch (start us, length us, event | category | flops | bytes accessed | tf_op | source)
XLA Modules:
  0.0 1815.5 jit_solution(9515872402518321086)
XLA Ops:
  7.9 4.4 collective-permute-start
  14.7 1.2 reduce-window.14
  16.3 1.0 copy.91
  17.3 1.0 maximum_convert_fusion
  18.3 1.0 multiply_convert_fusion
  20.6 373.6 %all-gather.2 = f32[64,1,4]{2,1,0:T(1,128)S(1)} all-gather(f32[1,1,4]{2,1,0:T(1,128)S(1)} %bitcast.179), channel_id=1, replica_groups=mesh['ctx'=64,'dp'=16] {'ctx'}, dimensions={0}, use_global_device_ids=true | all-gather | bytes 1040 | tf_op jit(solution)/shard_map/all_gather | solution.py:19
  394.5 342.9 %all-gather.6.cloned.1.call-done = f32[256,64,128]{2,1,0:T(8,128)} async-done(((f32[4,64,128]{2,1,0:T(8,128)}), f32[256,64,128]{2,1,0:T(8,128)}) %all-gather.6.cloned.1.call-update) | async-done | bytes 8388624 | tf_op jit(solution)/shard_map/all_gather | solution.py:19
  737.4 65.7 %while.28 = (s32[]{:T(128)}, f32[4,64,128]{2,1,0:T(8,128)S(1)}, s32[]{:T(128)}, f32[64,4,64,128]{3,2,1,0:T(8,128)}, f32[64,4]{1,0:T(8,128)S(1)}, /*index=5*/s32[]{:T(128)}, s32[]{:T(128)}, s32[]{:T(128)}, s32[]{:T(128)}) while((s32[]{:T(128)}, f32[4,64,128]{2,1,0:T(8,128)S(1)}, s32[]{:T(128)}, f32[64,4,64,128]{3,2,1,0:T(8,128)}, ...), condition=%wide.region_3.4_spmd, body=%wide.region_2.3_spmd.sunk | while | flops 65542 | bytes 393411 | solution.py:28
  737.5 1.0 bitcast_add_fusion.7
  740.6 1.0 bitcast_add_fusion.7
  743.7 1.0 bitcast_add_fusion.7
  744.8 1.0 bitcast_add_fusion.7
  747.9 1.0 bitcast_add_fusion.7
  748.9 1.0 bitcast_add_fusion.7
  752.0 1.0 bitcast_add_fusion.7
  753.1 1.0 bitcast_add_fusion.7
  756.2 1.0 bitcast_add_fusion.7
  757.3 1.0 bitcast_add_fusion.7
  760.4 1.0 bitcast_add_fusion.7
  763.5 1.0 bitcast_add_fusion.7
  764.5 1.0 bitcast_add_fusion.7
  767.7 1.0 bitcast_add_fusion.7
  768.7 1.0 bitcast_add_fusion.7
  771.8 1.0 bitcast_add_fusion.7
  772.9 1.0 bitcast_add_fusion.7
  776.0 1.0 bitcast_add_fusion.7
  777.1 1.0 bitcast_add_fusion.7
  780.2 1.0 bitcast_add_fusion.7
  808.2 730.4 %all-gather.8.cloned.1.call-done = f32[256,64,128]{2,1,0:T(8,128)} async-done(((f32[4,64,128]{2,1,0:T(8,128)}), f32[256,64,128]{2,1,0:T(8,128)}) %all-gather.8.cloned.1.call-update) | async-done | bytes 8388624 | tf_op jit(solution)/shard_map/all_gather | solution.py:19
  1541.4 1.2 reduce-window.16
  1544.0 1.3 collective-permute-start.1
  1545.4 262.4 %all-reduce.4 = (f32[4,512]{1,0:T(4,128)}, f32[512]{0:T(512)}, f32[4]{0:T(128)}, f32[4]{0:T(128)}, f32[4]{0:T(128)}) all-reduce(f32[4,512]{1,0:T(4,128)S(1)} %pad_maximum_fusion.1, f32[512]{0:T(512)S(1)} %get-tuple-element.183, f32[4]{0:T(128)S(1)} %get-tuple-element.211, ...), channel_id=1, replica_groups=mesh['ctx'=64,'dp'=16] {'ctx','dp'}, use_global_device_ids=true, to_apply=%region_20.21 | all-reduce | flops 2572 | bytes 20576 | tf_op jit(solution)/shard_map/psum | solution.py:56
  (189 shorter events, 58.6 us)
Async XLA Ops:
  7.2 797.5 %copy-start = (bf16[1,256,256]{2,1,0:T(8,128)(2,1)S(1)}, bf16[1,256,256]{2,1,0:T(8,128)(2,1)}, u32[]{:S(2)}) copy-start(bf16[1,256,256]{2,1,0:T(8,128)(2,1)} %param.23) | copy-start | bytes 393220
  7.2 798.9 %copy-start.4 = (f32[4]{0:T(128)S(1)}, f32[4]{0:T(128)}, u32[]{:S(2)}) copy-start(f32[4]{0:T(128)} %param.22) | copy-start | bytes 52
  7.2 730.2 %all-gather.6.cloned.1.call-start = ((), (), s32[]{:S(2)}) async-start(), calls=%async_computation | async-start | bytes 8519680 | tf_op jit(solution)/shard_map/all_gather | solution.py:19
  7.9 9.3 collective-permute-start
  20.3 1518.3 %all-gather.8.cloned.1.call-start = ((), (), s32[]{:S(2)}) async-start(), calls=%async_computation.1 | async-start | bytes 8519680 | tf_op jit(solution)/shard_map/all_gather | solution.py:19
  807.0 736.2 %copy-start.2 = (f32[1,256,4]{1,2,0:T(4,128)S(1)}, f32[1,256,4]{1,2,0:T(4,128)}, u32[]{:S(2)}) copy-start(f32[1,256,4]{1,2,0:T(4,128)} %param.19) | copy-start | bytes 12292
  807.0 736.2 %copy-start.3 = (f32[4]{0:T(128)S(1)}, f32[4]{0:T(128)}, u32[]{:S(2)}) copy-start(f32[4]{0:T(128)} %param.20) | copy-start | bytes 52
  807.0 737.0 %copy-start.5 = (f32[4]{0:T(128)S(1)}, f32[4]{0:T(128)}, u32[]{:S(2)}) copy-start(f32[4]{0:T(128)} %param.21) | copy-start | bytes 52
  1544.0 263.8 %collective-permute-start.1 = (f32[3,512]{1,0:T(4,128)S(1)}, f32[3,512]{1,0:T(4,128)S(1)}, u32[]{:S(2)}, u32[]{:S(2)}) collective-permute-start(f32[3,512]{1,0:T(4,128)S(1)} %pad_add_fusion.1), channel_id=1, source_target_pairs={{16,0},{32,16},{48,32},{64,48},{80,64},{96,80},{112,96},{128,112},... | collective-permute-start | bytes 18440 | tf_op jit(solution)/shard_map/ppermute | solution.py:34
  1808.0 0.7 copy-start.1
Sparse Core Ops, SparseCore 0:
  20.4 716.9 all-gather.5
  804.6 733.8 all-gather.7
where the time goes:
time: 1820 us
  waiting for transfers between devices  1070 us (59%)
  blocking collectives  636 us (35%)
  other arithmetic  71.4 us (4%)
    all_gather x2, waiting for transfers between devices, prefix(): gathered = jax.tree.map(lambda a: lax.all_gather(a, axis), part)  1070 us
    all_gather x1, blocking collectives, prefix(): gathered = jax.tree.map(lambda a: lax.all_gather(a, axis), part)  374 us
    psum x1, blocking collectives, reduce_grads(): lax.psum((weight_grad, bias_grad, grad_bias, grad_alog, skip_grad), ('ctx...  262 us
    add x63, other arithmetic, chain_step(): later[1] + later[0][:, None, None] * earlier[1]  62.7 us
  transfers between devices with their start and end apart: 4, of which 2 were waited for; matrix products, arithmetic and copies ran while one was open for 1% of the time, Pallas kernels for 0%

commit v1 on v0

v1 whole, which is shorter than its diff:
```python
import functools

import jax
import jax.numpy as jnp
from jax import lax
from jax.experimental import pallas as pl
from jax.experimental.pallas import tpu as pltpu
from jax.sharding import PartitionSpec as P

H = 4
P_SIZE = 64
N = 128
K = 4
L = 256
CH = 512
INNER = H * P_SIZE
NZ = 16
NX = 4
NC = 4
RC = N // NC
F32 = jnp.float32
BF16 = jnp.bfloat16
MESH = pl.DeviceIdType.MESH


def dot(a, b):
    return lax.dot_general(a, b, (((1,), (0,)), ((), ())), preferred_element_type=F32)


def dot_nt(a, b):
    return lax.dot_general(a, b, (((1,), (1,)), ((), ())), preferred_element_type=F32)


def dot_tn(a, b):
    return lax.dot_general(a, b, (((0,), (0,)), ((), ())), preferred_element_type=F32)


def split(a):
    hi = a.astype(BF16)
    return hi, (a - hi.astype(F32)).astype(BF16)


def split3(a):
    hi = a.astype(BF16)
    rest = a - hi.astype(F32)
    mid = rest.astype(BF16)
    return hi, mid, (rest - mid.astype(F32)).astype(BF16)


def iota(shape, dim):
    return lax.broadcasted_iota(jnp.int32, shape, dim)


def head_column(ref):
    rows = iota((8, 1), 0)
    col = jnp.zeros((8, 1), F32)
    for h in range(H):
        col = jnp.where(rows == h, ref[h], col)
    return col


def spread(cols, first):
    rows = cols.shape[0]
    low = iota((rows, 128), 1) < P_SIZE
    tiles = []
    for j in range(2):
        a = jnp.broadcast_to(cols[:, first + 2 * j : first + 2 * j + 1], (rows, 128))
        b = jnp.broadcast_to(cols[:, first + 2 * j + 1 : first + 2 * j + 2], (rows, 128))
        tiles.append(jnp.where(low, a, b))
    return jnp.concatenate(tiles, axis=1)


def head_rows(dtype):
    return (iota((8, INNER), 1) // P_SIZE == iota((8, INNER), 0)).astype(dtype)


def head_sums(x):
    sel = head_rows(F32).astype(BF16)
    hi, lo = split(x)
    return dot_nt(sel, hi) + dot_nt(sel, lo)


def main_kernel(
    dt_bias_ref, a_log_ref, skip_ref, raw_ref, halo_ref, w_ref, bias_ref, dt_ref, cot_ref,
    gx_ref, tail_ref, spill_ref, gpre_ref, sums_ref,
    xp, pre_s, sig_s, xb, rows_s, cols_s, loc, dec, tw_e, up_e, st_e, ac, gbl, gcl, pair_s,
    gc_pad, rbuf, sbuf, xsend, xrecv, s_in, g_after,
    send_sem, recv_sem, xsend_sem, xrecv_sem,
):
    place = lax.axis_index("ctx")
    dp = lax.axis_index("dp")
    z = lax.rem(place, NZ)
    x = place // NZ
    barrier = pltpu.get_barrier_semaphore()

    @pl.when(z > 0)
    def _():
        pl.semaphore_signal(barrier, inc=1, device_id=(place - 1, dp), device_id_type=MESH)

    @pl.when(z < NZ - 1)
    def _():
        pl.semaphore_signal(barrier, inc=1, device_id=(place + 1, dp), device_id_type=MESH)

    for k in range(1, NX):
        pl.semaphore_signal(
            barrier, inc=1, device_id=(lax.rem(place + k * NZ, NX * NZ), dp), device_id_type=MESH
        )

    xp[0:8, :] = halo_ref[...].astype(F32)
    xp[8 : 8 + L, :] = raw_ref[...].astype(F32)
    for r in range(0, L, 64):
        pre = bias_ref[...] + sum(
            w_ref[k : k + 1, :] * xp[5 + k + r : 5 + k + r + 64, :] for k in range(K)
        )
        sig = 1.0 / (1.0 + jnp.exp(-pre))
        pre_s[r : r + 64, :] = pre
        sig_s[r : r + 64, :] = sig
        xb[r : r + 64, :] = (pre * sig).astype(BF16)

    rate = -jnp.exp(head_column(a_log_ref))
    live = iota((8, 1), 0) < H
    rate = jnp.where(live, rate, 0.0)
    rows_s[...] = jnp.zeros_like(rows_s)
    rows_s[0:H, :] = dt_ref[...]
    dt_pre = rows_s[0:8, :] + head_column(dt_bias_ref)
    step = jnp.where(
        live, jnp.maximum(dt_pre, 0.0) + jnp.log1p(jnp.exp(-jnp.abs(dt_pre))), 0.0
    )
    upto = (iota((L, L), 0) <= iota((L, L), 1)).astype(F32).astype(BF16)
    cum = sum(dot(part, upto) for part in split3(step * rate))
    cum_last = cum[:, L - 1 : L]
    to_end = jnp.exp(cum_last - cum)
    tw = to_end * step
    up = jnp.exp(cum)
    rows_s[0:8, :] = cum
    rows_s[8:16, :] = step
    rows_s[16:24, :] = tw
    rows_s[24:32, :] = up
    cols = jnp.transpose(rows_s[...])
    cols_s[...] = cols
    tw_e[...] = spread(cols, 16)
    up_e[...] = spread(cols, 24)
    st_e[...] = spread(cols, 8)
    decay_lanes = up_e[L - 1 : L, :]
    dec[...] = jnp.broadcast_to(decay_lanes, (8, INNER))

    b_val = xb[:, INNER : INNER + N]
    c_val = xb[:, INNER + N :]
    hi, lo = split(xb[:, :INNER].astype(F32) * tw_e[...])
    loc[0] = dot_tn(b_val, hi) + dot_tn(b_val, lo)
    hi, lo = split(cot_ref[...].astype(F32) * up_e[...])
    loc[1] = dot_tn(c_val, hi) + dot_tn(c_val, lo)

    @pl.when(z == 0)
    def _():
        rbuf[0, :, 0 : 2 * RC, :] = jnp.zeros((NC, 2 * RC, INNER), F32)
        rbuf[0, :, 2 * RC :, :] = jnp.ones((NC, 8, INNER), F32)

    @pl.when(z == NZ - 1)
    def _():
        rbuf[1, :, 0 : 2 * RC, :] = jnp.zeros((NC, 2 * RC, INNER), F32)
        rbuf[1, :, 2 * RC :, :] = jnp.ones((NC, 8, INNER), F32)

    pl.semaphore_wait(
        barrier, NX - 1 + (z > 0).astype(jnp.int32) + (z < NZ - 1).astype(jnp.int32)
    )

    first = (z >= NZ // 2).astype(jnp.int32)

    def hop(way, c):
        nearer = place + 1 - 2 * way
        return pltpu.make_async_remote_copy(
            src_ref=sbuf.at[way, c],
            dst_ref=rbuf.at[way, c],
            send_sem=send_sem.at[way, c],
            recv_sem=recv_sem.at[way, c],
            device_id=(nearer, dp),
            device_id_type=MESH,
        )

    def has_in(way):
        return jnp.where(way == 0, z, NZ - 1 - z) > 0

    def has_out(way):
        return jnp.where(way == 0, NZ - 1 - z, z) > 0

    def relay(way, c):
        @pl.when(has_in(way))
        def _():
            hop(way, c).wait_recv()

        @pl.when(has_out(way))
        def _():
            rows = pl.ds(pl.multiple_of(c * RC, RC), RC)
            d = dec[0:1, :]
            main = rbuf[way, c, 0:RC, :]
            aux = rbuf[way, c, RC : 2 * RC, :]
            factor = rbuf[way, c, 2 * RC :, :]
            sbuf[way, c, 0:RC, :] = d * main + loc[way, rows, :]
            sbuf[way, c, RC : 2 * RC, :] = aux + factor[0:1, :] * loc[1 - way, rows, :]
            sbuf[way, c, 2 * RC :, :] = factor * dec[...]
            hop(way, c).start()

    def cross(k, c, kind):
        other = lax.rem(x + k, NX)
        return pltpu.make_async_remote_copy(
            src_ref=xsend.at[kind, c],
            dst_ref=xrecv.at[x, c],
            send_sem=xsend_sem.at[k - 1, c],
            recv_sem=xrecv_sem.at[x, c],
            device_id=(other * NZ + z, dp),
            device_id_type=MESH,
        )

    def arrival(k, c):
        source = lax.rem(x + k, NX)
        return pltpu.make_async_remote_copy(
            src_ref=xsend.at[0, c],
            dst_ref=xrecv.at[source, c],
            send_sem=xsend_sem.at[k - 1, c],
            recv_sem=xrecv_sem.at[source, c],
            device_id=(source * NZ + z, dp),
            device_id_type=MESH,
        )

    def exchange(c):
        rows = pl.ds(pl.multiple_of(c * RC, RC), RC)
        d = dec[0:1, :]
        f = rbuf[0, c, 2 * RC :, :]
        e = rbuf[1, c, 2 * RC :, :]
        xsend[0, c, 0:RC, :] = (
            e[0:1, :] * (d * rbuf[0, c, 0:RC, :] + loc[0, rows, :]) + rbuf[1, c, RC : 2 * RC, :]
        )
        xsend[1, c, 0:RC, :] = (
            f[0:1, :] * (d * rbuf[1, c, 0:RC, :] + loc[1, rows, :]) + rbuf[0, c, RC : 2 * RC, :]
        )
        whole = f * e * dec[...]
        xsend[0, c, RC:, :] = whole
        xsend[1, c, RC:, :] = whole
        for k in range(1, NX):
            other = lax.rem(x + k, NX)
            cross(k, c, (other < x).astype(jnp.int32)).start()

    def relay_first(c, _):
        relay(first, c)
        return 0

    def relay_second(c, _):
        relay(1 - first, c)
        exchange(c)
        return 0

    early = jnp.logical_or(z < 4, z >= NZ - 4)

    @pl.when(early)
    def _():
        lax.fori_loop(0, NC, relay_first, 0)

    pair_s[...] = jnp.zeros_like(pair_s)
    low = iota((128, 128), 1) < P_SIZE
    for sb in range(2):
        t0 = 128 * sb
        wide = L - t0
        rs = slice(t0, t0 + 128)
        gram = dot_nt(xb[rs, INNER : INNER + N], xb[t0:, INNER + N :])
        mask = iota((128, wide), 1) >= iota((128, wide), 0)
        dgram = jnp.zeros((128, wide), F32)
        for j in range(2):
            cot_t = cot_ref[t0:, 128 * j : 128 * j + 128]
            v_t = xb[rs, 128 * j : 128 * j + 128]
            parts = []
            for i in range(2):
                h = 2 * j + i
                keep = low if i == 0 else jnp.logical_not(low)
                v_h = jnp.where(keep, v_t.astype(F32), 0.0).astype(BF16)
                gap = rows_s[h : h + 1, t0:] - cols_s[rs, h : h + 1]
                within = jnp.exp(jnp.where(mask, gap, -1e30))
                dmix = dot_nt(v_h, cot_t)
                hi, lo = split(gram * within)
                parts.append(dot(hi, cot_t) + dot(lo, cot_t))
                dw = dmix * within * cols_s[rs, 8 + h : 9 + h]
                dgram = dgram + dw
                pair_s[h : h + 1, t0:] += jnp.sum(dw * gram, axis=0, keepdims=True)
            ac[rs, 128 * j : 128 * j + 128] = jnp.where(low, parts[0], parts[1])
        hi, lo = split(dgram)
        c_t = xb[t0:, INNER + N :]
        b_s = xb[rs, INNER : INNER + N]
        gbl[rs, :] = dot(hi, c_t) + dot(lo, c_t)
        from_here = dot_tn(hi, b_s) + dot_tn(lo, b_s)
        if sb == 0:
            gcl[...] = from_here
        else:
            gcl[t0:, :] += from_here

    @pl.when(jnp.logical_not(early))
    def _():
        lax.fori_loop(0, NC, relay_first, 0)

    lax.fori_loop(0, NC, relay_second, 0)

    def gather(c, _):
        for k in range(1, NX):
            arrival(k, c).wait_recv()
        s_in[pl.ds(pl.multiple_of(c * RC, RC), RC), :] = jnp.zeros((RC, INNER), F32)
        g_after[pl.ds(pl.multiple_of(c * RC, RC), RC), :] = jnp.zeros((RC, INNER), F32)
        rows = pl.ds(pl.multiple_of(c * RC, RC), RC)
        for k in range(NX - 1):

            @pl.when(k < x)
            def _():
                s_in[rows, :] = xrecv[k, c, RC : RC + 1, :] * s_in[rows, :] + xrecv[k, c, 0:RC, :]

        for k in range(NX - 1, 0, -1):

            @pl.when(k > x)
            def _():
                g_after[rows, :] = (
                    xrecv[k, c, RC : RC + 1, :] * g_after[rows, :] + xrecv[k, c, 0:RC, :]
                )

        s_in[rows, :] = rbuf[0, c, 0:RC, :] + rbuf[0, c, 2 * RC : 2 * RC + 1, :] * s_in[rows, :]
        g_after[rows, :] = (
            rbuf[1, c, 0:RC, :] + rbuf[1, c, 2 * RC : 2 * RC + 1, :] * g_after[rows, :]
        )
        return 0

    lax.fori_loop(0, NC, gather, 0)

    b_val = xb[:, INNER : INNER + N]
    c_val = xb[:, INNER + N :]
    s_hi, s_lo = split(s_in[...])
    g_hi, g_lo = split(g_after[...])
    state_back = dot(b_val, g_hi) + dot(b_val, g_lo)
    state_proj = dot(c_val, s_hi) + dot(c_val, s_lo)
    cot = cot_ref[...].astype(F32)
    vals = xb[:, :INNER].astype(F32)
    scaled = cot * up_e[...]
    hi, lo = split(scaled)
    grad_c = gcl[...] + dot_nt(hi, s_hi) + dot_nt(hi, s_lo) + dot_nt(lo, s_hi)
    hi, lo = split(vals * tw_e[...])
    grad_b = gbl[...] + dot_nt(hi, g_hi) + dot_nt(hi, g_lo) + dot_nt(lo, g_hi)
    local_step = head_sums(vals * ac[...])
    tail_grad = head_sums(vals * state_back)
    proj_term = head_sums(scaled * state_proj)
    skip_lanes = spread(jnp.broadcast_to(0.0, (8, 128)) + sum(
        jnp.where(iota((8, 128), 1) == h, skip_ref[h], 0.0) for h in range(H)
    ), 0)[0:1, :]
    grad_vals = st_e[...] * ac[...] + skip_lanes * cot + tw_e[...] * state_back

    step = rows_s[8:16, :]
    tw = rows_s[16:24, :]
    cum = rows_s[0:8, :]
    cum_last = cum[:, L - 1 : L]
    sel = head_rows(F32)
    skip_sum = jnp.sum(sel * jnp.sum(cot * vals, axis=0, keepdims=True), axis=1, keepdims=True)
    both = jnp.sum(
        sel * jnp.sum(s_in[...] * g_after[...], axis=0, keepdims=True), axis=1, keepdims=True
    )
    tail_term = tail_grad * tw
    extra = jnp.sum(tail_term, axis=1, keepdims=True) + jnp.exp(cum_last) * both
    grad_cum = pair_s[...] - step * local_step + proj_term - tail_term
    since = (iota((L, L), 0) >= iota((L, L), 1)).astype(F32).astype(BF16)
    grad_log = sum(dot(part, since) for part in split3(grad_cum)) + extra
    rows_s[32 : 32 + H, :] = dt_ref[...]
    dt_pre = rows_s[32:40, :] + head_column(dt_bias_ref)
    rate = -jnp.exp(head_column(a_log_ref))
    grad_step = local_step + tail_grad * jnp.exp(cum_last - cum) + rate * grad_log
    grad_pre = grad_step / (1.0 + jnp.exp(-dt_pre))
    gpre_ref[...] = grad_pre[0:H, :]
    alog_sum = rate * jnp.sum(grad_log * step, axis=1, keepdims=True)
    bias_sum = jnp.sum(grad_pre, axis=1, keepdims=True)

    gc_pad[0:8, :] = jnp.zeros((8, CH), F32)
    gc_pad[8 + L : 16 + L, :] = jnp.zeros((8, CH), F32)
    for lanes, value in (
        (slice(0, INNER), grad_vals),
        (slice(INNER, INNER + N), grad_b),
        (slice(INNER + N, CH), grad_c),
    ):
        low_value = value.astype(BF16).astype(F32)
        sig = sig_s[:, lanes]
        gc_pad[8 : 8 + L, lanes] = low_value * sig * (1.0 + pre_s[:, lanes] * (1.0 - sig))

    spill_ref[...] = sum(w_ref[k : k + 1, :] * gc_pad[3 - k : 11 - k, :] for k in range(K))
    sums_ref[...] = jnp.zeros_like(sums_ref)
    for r in range(0, L, 64):
        rows = sum(
            w_ref[k : k + 1, :] * gc_pad[11 - k + r : 11 - k + r + 64, :] for k in range(K)
        )
        gx_ref[r : r + 64, :] = rows.astype(BF16)
        if r + 64 == L:
            tail_ref[...] = rows[56:64, :]
    for k in range(K + 1):
        term = gc_pad[8 : 8 + L, :]
        if k < K:
            term = term * xp[5 + k : 5 + k + L, :]
        total = jnp.sum(term, axis=0, keepdims=True)
        for j in range(4):
            sums_ref[4 * k + j] = total[:, 128 * j : 128 * j + 128]
    lane = iota((8, 128), 1)
    row = iota((8, 128), 0)
    small = (
        jnp.where(lane == row, bias_sum, 0.0)
        + jnp.where(lane == row + 8, alog_sum, 0.0)
        + jnp.where(lane == row + 16, skip_sum, 0.0)
    )
    small = jnp.where(row < H, small, 0.0)
    sums_ref[20] = jnp.sum(small, axis=0, keepdims=True)

    def drain(c, _):
        for way in range(2):

            @pl.when(has_out(way))
            def _():
                hop(way, c).wait_send()

        for k in range(1, NX):
            arrival(k, c).wait_send()
        return 0

    lax.fori_loop(0, NC, drain, 0)


def run_main(raw, halo, weight, bias, dt_t, dt_bias, a_log, d_skip, cot):
    vmem = pl.BlockSpec(memory_space=pltpu.VMEM)
    smem = pl.BlockSpec(memory_space=pltpu.SMEM)
    return pl.pallas_call(
        main_kernel,
        out_shape=(
            jax.ShapeDtypeStruct((L, CH), BF16),
            jax.ShapeDtypeStruct((8, CH), F32),
            jax.ShapeDtypeStruct((8, CH), F32),
            jax.ShapeDtypeStruct((H, L), F32),
            jax.ShapeDtypeStruct((32, 1, 128), F32),
        ),
        in_specs=[smem] * 3 + [vmem] * 6,
        out_specs=(vmem,) * 5,
        scratch_shapes=[
            pltpu.VMEM((8 + L, CH), F32),
            pltpu.VMEM((L, CH), F32),
            pltpu.VMEM((L, CH), F32),
            pltpu.VMEM((L, CH), BF16),
            pltpu.VMEM((128, L), F32),
            pltpu.VMEM((L, 128), F32),
            pltpu.VMEM((2, N, INNER), F32),
            pltpu.VMEM((8, INNER), F32),
            pltpu.VMEM((L, INNER), F32),
            pltpu.VMEM((L, INNER), F32),
            pltpu.VMEM((L, INNER), F32),
            pltpu.VMEM((L, INNER), F32),
            pltpu.VMEM((L, N), F32),
            pltpu.VMEM((L, N), F32),
            pltpu.VMEM((8, L), F32),
            pltpu.VMEM((16 + L, CH), F32),
            pltpu.VMEM((2, NC, 2 * RC + 8, INNER), F32),
            pltpu.VMEM((2, NC, 2 * RC + 8, INNER), F32),
            pltpu.VMEM((2, NC, RC + 8, INNER), F32),
            pltpu.VMEM((NX, NC, RC + 8, INNER), F32),
            pltpu.VMEM((N, INNER), F32),
            pltpu.VMEM((N, INNER), F32),
            pltpu.SemaphoreType.DMA((2, NC)),
            pltpu.SemaphoreType.DMA((2, NC)),
            pltpu.SemaphoreType.DMA((NX - 1, NC)),
            pltpu.SemaphoreType.DMA((NX, NC)),
        ],
        compiler_params=pltpu.CompilerParams(
            collective_id=0, has_side_effects=True, vmem_limit_bytes=48 << 20
        ),
        name="slab",
    )(dt_bias, a_log, d_skip, raw, halo, weight, bias, dt_t, cot)


NY = 4
NR = 32
ZR = 32


def reduce_kernel(in_ref, out_ref, plane, line, own, send_sem, recv_sem):
    place = lax.axis_index("ctx")
    dp = lax.axis_index("dp")
    z_lo = lax.rem(place, NZ)
    x = place // NZ
    y = dp // 4
    z_hi = lax.rem(dp // 2, 2)
    core = lax.rem(dp, 2)
    me = (x * NY + y) * 2 + core
    z = z_hi * NZ + z_lo

    def in_plane(r):
        rx = r // 8
        ry = lax.rem(r // 2, NY)
        rc = lax.rem(r, 2)
        return (rx * NZ + z_lo, ry * 4 + z_hi * 2 + rc)

    def in_line(q):
        return (x * NZ + lax.rem(q, NZ), y * 4 + (q // NZ) * 2 + core)

    barrier = pltpu.get_barrier_semaphore()

    def greet(k, _):
        pl.semaphore_signal(
            barrier, inc=1, device_id=in_plane(lax.rem(me + k, NR)), device_id_type=MESH
        )
        pl.semaphore_signal(
            barrier, inc=1, device_id=in_line(lax.rem(z + k, ZR)), device_id_type=MESH
        )
        return 0

    lax.fori_loop(1, NR, greet, 0)
    plane[pl.ds(me, 1)] = in_ref[pl.ds(me, 1)]
    pl.semaphore_wait(barrier, NR - 1 + ZR - 1)

    def send(src, dst, stage, target):
        return pltpu.make_async_remote_copy(
            src_ref=src,
            dst_ref=dst,
            send_sem=send_sem.at[stage],
            recv_sem=recv_sem.at[stage],
            device_id=target,
            device_id_type=MESH,
        )

    def all_of(buf, stage):
        return pltpu.make_async_remote_copy(
            src_ref=buf.at[pl.ds(0, NR - 1)],
            dst_ref=buf.at[pl.ds(0, NR - 1)],
            send_sem=send_sem.at[stage],
            recv_sem=recv_sem.at[stage],
            device_id=in_plane(lax.rem(me + 1, NR)),
            device_id_type=MESH,
        )

    def scatter(k, _):
        r = lax.rem(me + k, NR)
        send(in_ref.at[r], plane.at[me], 0, in_plane(r)).start()
        return 0

    lax.fori_loop(1, NR, scatter, 0)
    all_of(plane, 0).wait_recv()
    mine = jnp.sum(plane[...], axis=0, keepdims=True)
    own[0:1] = mine
    line[pl.ds(z, 1)] = mine

    def along(k, _):
        q = lax.rem(z + k, ZR)
        send(own.at[0], line.at[z], 1, in_line(q)).start()
        return 0

    lax.fori_loop(1, ZR, along, 0)
    all_of(line, 1).wait_recv()
    total = jnp.sum(line[...], axis=0, keepdims=True)
    own[1:2] = total
    out_ref[pl.ds(me, 1)] = total

    def spread_out(k, _):
        send(own.at[1], out_ref.at[me], 2, in_plane(lax.rem(me + k, NR))).start()
        return 0

    lax.fori_loop(1, NR, spread_out, 0)
    all_of(out_ref, 2).wait_recv()
    for stage, buf in enumerate((plane, line, out_ref)):
        all_of(buf, stage).wait_send()


def run_reduce(sums):
    vmem = pl.BlockSpec(memory_space=pltpu.VMEM)
    return pl.pallas_call(
        reduce_kernel,
        out_shape=jax.ShapeDtypeStruct((32, 1, 128), F32),
        in_specs=[vmem],
        out_specs=vmem,
        scratch_shapes=[
            pltpu.VMEM((NR, 1, 128), F32),
            pltpu.VMEM((ZR, 1, 128), F32),
            pltpu.VMEM((2, 1, 128), F32),
            pltpu.SemaphoreType.DMA((3,)),
            pltpu.SemaphoreType.DMA((3,)),
        ],
        compiler_params=pltpu.CompilerParams(collective_id=1, has_side_effects=True),
        name="totals",
    )(sums)


def shift(block, axis, distance):
    devices = range(lax.axis_size(axis))
    route = [(i - distance, i) for i in devices if i - distance in devices]
    return lax.ppermute(block, axis, route)


def on_device(xbc_raw, conv_weight, conv_bias, dt_raw, dt_bias, a_log, d_skip, grad_out):
    raw = xbc_raw[0]
    halo = shift(raw[L - 8 :], "ctx", 1)
    gx, tail, spill, gpre, sums = run_main(
        raw, halo, conv_weight, conv_bias[None], dt_raw[0].T, dt_bias, a_log, d_skip, grad_out[0]
    )
    back = shift(spill[5:], "ctx", -1)
    totals = run_reduce(sums)
    last = jnp.concatenate([tail[:5], tail[5:] + back], 0).astype(BF16)
    grad_input = lax.dynamic_update_slice(gx, last, (L - 8, 0))[None]
    weight_grad = totals[:16].reshape(K, CH)
    bias_grad = totals[16:20].reshape(CH)
    small = totals[20, 0]
    return (
        grad_input, gpre.T[None], weight_grad, bias_grad, small[0:4], small[8:12], small[16:20],
    )


def solution(mesh):
    rows = P("dp", "ctx", None)
    return jax.shard_map(
        on_device,
        mesh=mesh,
        in_specs=(rows, P(), P(), rows, P(), P(), P(), rows),
        out_specs=(rows, rows, P(), P(), P(), P(), P()),
        check_vma=False,
    )
```

time: 1820 us -> 160 us (0.09)
  the two profiles are of different devices: /device:TPU:1 before, /device:TPU:2 now
where the time goes in v1:
time: 160 us; the launch traced here: 159 us
  Pallas kernels  111 us (69%)
  waiting for transfers between devices  24.2 us (15%)
  starting transfers between devices  14.4 us (9%)
  local copies, waits for them, and re-layouts  9.04 us (6%)
    pallas_call x1, Pallas kernels, run_main(): pl.pallas_call(main_kernel, out_shape=(jax.ShapeDtypeStruct((L, CH), BF16...  64.4 us
    pallas_call x1, Pallas kernels, run_reduce(): pl.pallas_call(reduce_kernel, out_shape=jax.ShapeDtypeStruct((32, 1, 128)...  46.7 us
    ppermute x2, waiting for transfers between devices, shift(): return lax.ppermute(block, axis, route)  24.2 us
    ppermute x2, starting transfers between devices, shift(): return lax.ppermute(block, axis, route)  14.4 us
    unnamed x20, local copies, waits for them, and re-layouts  4.41 us
  transfers between devices with their start and end apart: 2, of which 1 were waited for; matrix products, arithmetic and copies ran while one was open for 2% of the time, Pallas kernels for 0%

profile of v1, /device:TPU:2, one launch (start us, length us, event | category | flops | bytes accessed | tf_op | source)
XLA Modules:
  0.0 159.5 jit_solution(767346376287892823)
XLA Ops:
  0.6 0.0 copy-start.3
  0.6 0.7 slice_bitcast_fusion
  1.3 0.0 copy-start.4
  1.3 3.9 %collective-permute-start = (bf16[8,512]{1,0:T(8,128)(2,1)S(1)}, bf16[8,512]{1,0:T(8,128)(2,1)S(1)}, u32[]{:S(2)}, u32[]{:S(2)}) collective-permute-start(bf16[8,512]{1,0:T(8,128)(2,1)S(1)} %slice_bitcast_fusion), channel_id=1, source_target_pairs={{0,16},{16,32},{32,48},{48,64},{64,80},{80,96},{96,112},{112,128},... | collective-permute-start | bytes 24584 | tf_op jit(solution)/shard_map/ppermute | solution.py:587
  5.3 24.2 %collective-permute-done.halo_ref = bf16[8,512]{1,0:T(8,128)(2,1)S(1)} collective-permute-done((bf16[8,512]{1,0:T(8,128)(2,1)S(1)}, bf16[8,512]{1,0:T(8,128)(2,1)S(1)}, u32[]{:S(2)}, u32[]{:S(2)}) %collective-permute-start) | collective-permute-done | bytes 8224 | tf_op jit(solution)/shard_map/ppermute | solution.py:587
  29.5 0.0 copy-start.5
  29.5 0.0 copy-start.6
  29.5 0.0 copy-start.7
  29.5 0.0 copy-start.8
  29.5 0.0 copy-done.3
  29.5 0.0 copy-done.4
  29.5 0.7 copy-done.5
  30.2 0.0 copy-done.6
  30.2 0.0 copy-done.7
  30.2 0.0 copy-done.8
  30.2 0.0 copy-start
  30.2 0.9 copy-done
  31.1 0.0 copy-start.1
  31.1 0.9 copy-done.1
  32.0 64.4 %slab.1 = (bf16[256,512]{1,0:T(8,128)(2,1)S(1)}, f32[8,512]{1,0:T(8,128)S(1)}, f32[8,512]{1,0:T(8,128)S(1)}, f32[4,256]{1,0:T(4,128)S(1)}, f32[32,1,128]{2,1,0:T(1,128)S(1)}) custom-call(f32[4]{0:T(128)S(1)} %copy-done.6, f32[4]{0:T(128)S(1)} %copy-done.7, f32[4]{0:T(128)S(1)} %copy-done.8, bf16[256,512]{1,0:T(8,128)(2,1)S(1)} %bitcast.23, ...), custom_call_target="tpu_custom_call" | custom-call | tf_op jit(solution)/shard_map/slab/pallas_call | solution.py:427
  96.4 0.0 copy-start.2
  96.5 0.6 copy-done.2
  97.0 46.7 %totals.1 = f32[32,1,128]{2,1,0:T(1,128)} custom-call(f32[32,1,128]{2,1,0:T(1,128)} %copy-done.2), custom_call_target="tpu_custom_call" | custom-call | tf_op jit(solution)/shard_map/totals/pallas_call | solution.py:567
  143.8 1.3 slice_bitcast_fusion.1
  145.1 10.4 %collective-permute-start.1 = (f32[3,512]{1,0:T(4,128)S(1)}, f32[3,512]{1,0:T(4,128)S(1)}, u32[]{:S(2)}, u32[]{:S(2)}) collective-permute-start(f32[3,512]{1,0:T(4,128)S(1)} %slice.48), channel_id=1, source_target_pairs={{16,0},{32,16},{48,32},{64,48},{80,64},{96,80},{112,96},{128,112},... | collective-permute-start | bytes 18440 | tf_op jit(solution)/shard_map/ppermute | solution.py:587
  155.5 0.7 slice_reduce_fusion
  156.3 1.3 slice.50
  157.5 0.6 reshape.57
  158.1 0.0 collective-permute-done.1
  158.2 0.7 copy.18
  158.9 0.6 copy.19
  (4 shorter events, 0.0 us)
Async XLA Ops:
  0.6 28.9 %copy-start.3 = (f32[4,512]{1,0:T(4,128)S(1)}, f32[4,512]{1,0:T(4,128)}, u32[]{:S(2)}) copy-start(f32[4,512]{1,0:T(4,128)} %w_ref.1) | copy-start | bytes 24580
  1.3 28.1 %copy-start.4 = (f32[1,256,4]{1,2,0:T(4,128)S(1)}, f32[1,256,4]{1,2,0:T(4,128)}, u32[]{:S(2)}) copy-start(f32[1,256,4]{1,2,0:T(4,128)} %param.11) | copy-start | bytes 12292
  1.3 28.1 %collective-permute-start = (bf16[8,512]{1,0:T(8,128)(2,1)S(1)}, bf16[8,512]{1,0:T(8,128)(2,1)S(1)}, u32[]{:S(2)}, u32[]{:S(2)}) collective-permute-start(bf16[8,512]{1,0:T(8,128)(2,1)S(1)} %slice_bitcast_fusion), channel_id=1, source_target_pairs={{0,16},{16,32},{32,48},{48,64},{64,80},{80,96},{96,112},{112,128},... | collective-permute-start | bytes 24584 | tf_op jit(solution)/shard_map/ppermute | solution.py:587
  29.5 0.7 copy-start.5
  29.5 0.7 copy-start.6
  29.5 0.7 copy-start.7
  29.5 0.7 copy-start.8
  30.2 0.9 copy-start
  31.1 0.9 copy-start.1
  96.4 0.6 copy-start.2
  145.1 13.1 %collective-permute-start.1 = (f32[3,512]{1,0:T(4,128)S(1)}, f32[3,512]{1,0:T(4,128)S(1)}, u32[]{:S(2)}, u32[]{:S(2)}) collective-permute-start(f32[3,512]{1,0:T(4,128)S(1)} %slice.48), channel_id=1, source_target_pairs={{16,0},{32,16},{48,32},{64,48},{80,64},{96,80},{112,96},{128,112},... | collective-permute-start | bytes 18440 | tf_op jit(solution)/shard_map/ppermute | solution.py:587

commit v2 on v1

v2 whole, which is shorter than its diff:
```python
import functools

import jax
import jax.numpy as jnp
from jax import lax
from jax.experimental import pallas as pl
from jax.experimental.pallas import tpu as pltpu
from jax.sharding import PartitionSpec as P

H = 4
P_SIZE = 64
N = 128
K = 4
L = 256
CH = 512
INNER = H * P_SIZE
NZ = 16
NX = 4
NY = 4
NR = 32
ZR = 32
NC = 16
RC = N // NC
F32 = jnp.float32
BF16 = jnp.bfloat16
MESH = pl.DeviceIdType.MESH


def dot(a, b):
    return lax.dot_general(a, b, (((1,), (0,)), ((), ())), preferred_element_type=F32)


def dot_nt(a, b):
    return lax.dot_general(a, b, (((1,), (1,)), ((), ())), preferred_element_type=F32)


def dot_tn(a, b):
    return lax.dot_general(a, b, (((0,), (0,)), ((), ())), preferred_element_type=F32)


def split(a):
    hi = a.astype(BF16)
    return hi, (a - hi.astype(F32)).astype(BF16)


def split3(a):
    hi = a.astype(BF16)
    rest = a - hi.astype(F32)
    mid = rest.astype(BF16)
    return hi, mid, (rest - mid.astype(F32)).astype(BF16)


def iota(shape, dim):
    return lax.broadcasted_iota(jnp.int32, shape, dim)


def head_column(ref):
    rows = iota((8, 1), 0)
    col = jnp.zeros((8, 1), F32)
    for h in range(H):
        col = jnp.where(rows == h, ref[h], col)
    return col


def spread(cols, first):
    rows = cols.shape[0]
    low = iota((rows, 128), 1) < P_SIZE
    tiles = []
    for j in range(2):
        a = jnp.broadcast_to(cols[:, first + 2 * j : first + 2 * j + 1], (rows, 128))
        b = jnp.broadcast_to(cols[:, first + 2 * j + 1 : first + 2 * j + 2], (rows, 128))
        tiles.append(jnp.where(low, a, b))
    return jnp.concatenate(tiles, axis=1)


def head_rows(dtype):
    return (iota((8, INNER), 1) // P_SIZE == iota((8, INNER), 0)).astype(dtype)


def head_sums(x):
    sel = head_rows(F32).astype(BF16)
    hi, lo = split(x)
    return dot_nt(sel, hi) + dot_nt(sel, lo)


def main_kernel(
    dt_bias_ref, a_log_ref, skip_ref, halo_ref, raw_hbm, w_hbm, bias_hbm, dt_hbm, cot_hbm,
    gx_ref, gpre_ref, wg_ref, bg_ref, small_ref,
    raw_ref, w_ref, bias_ref, dt_ref, cot_ref, in_sem,
    xp, pre_s, sig_s, xb, rows_s, cols_s, loc, dec, tw_e, up_e, st_e, ac, gbl, gcl, pair_s,
    gc_pad, rbuf, sbuf, rfac, sfac, xsend, xrecv, xfac, xdec, s_in, g_after,
    spill_out, spill_in, sums_ref, plane, line, own, totals,
    send_sem, recv_sem, fsend_sem, frecv_sem, xsend_sem, xrecv_sem, ssend_sem, srecv_sem,
    rsend_sem, rrecv_sem, edge_sem, known_sem,
):
    place = lax.axis_index("ctx")
    dp = lax.axis_index("dp")
    z = lax.rem(place, NZ)
    x = place // NZ
    y = dp // 4
    z_hi = lax.rem(dp // 2, 2)
    core = lax.rem(dp, 2)

    def device(x_, y_, ring, core_):
        return (x_ * NZ + lax.rem(ring, NZ), y_ * 4 + (ring // NZ) * 2 + core_)

    ring = z_hi * NZ + z
    barrier = pltpu.get_barrier_semaphore()
    inputs = [
        pltpu.make_async_copy(src, dst, in_sem.at[i])
        for i, (src, dst) in enumerate(
            ((raw_hbm, raw_ref), (w_hbm, w_ref), (bias_hbm, bias_ref), (dt_hbm, dt_ref),
             (cot_hbm, cot_ref))
        )
    ]
    for copy in inputs:
        copy.start()
    for step in (1, ZR - 1):
        pl.semaphore_signal(
            barrier, inc=1, device_id=device(x, y, lax.rem(ring + step, ZR), core),
            device_id_type=MESH,
        )
    for k in range(1, NX):
        pl.semaphore_signal(
            barrier, inc=1, device_id=device(lax.rem(x + k, NX), y, ring, core),
            device_id_type=MESH,
        )
    for k in range(1, 2 * NY):
        q = lax.rem(y * 2 + core + k, 2 * NY)
        pl.semaphore_signal(
            barrier, inc=1, device_id=device(x, q // 2, ring, lax.rem(q, 2)), device_id_type=MESH
        )
    for copy in inputs:
        copy.wait()

    xp[0:8, :] = halo_ref[...].astype(F32)
    xp[8 : 8 + L, :] = raw_ref[...].astype(F32)
    for r in range(0, L, 64):
        pre = bias_ref[...] + sum(
            w_ref[k : k + 1, :] * xp[5 + k + r : 5 + k + r + 64, :] for k in range(K)
        )
        sig = 1.0 / (1.0 + jnp.exp(-pre))
        pre_s[r : r + 64, :] = pre
        sig_s[r : r + 64, :] = sig
        xb[r : r + 64, :] = (pre * sig).astype(BF16)

    rate = -jnp.exp(head_column(a_log_ref))
    live = iota((8, 1), 0) < H
    rate = jnp.where(live, rate, 0.0)
    rows_s[...] = jnp.zeros_like(rows_s)
    rows_s[0:H, :] = dt_ref[...]
    dt_pre = rows_s[0:8, :] + head_column(dt_bias_ref)
    step = jnp.where(
        live, jnp.maximum(dt_pre, 0.0) + jnp.log1p(jnp.exp(-jnp.abs(dt_pre))), 0.0
    )
    upto = (iota((L, L), 0) <= iota((L, L), 1)).astype(F32).astype(BF16)
    cum = sum(dot(part, upto) for part in split3(step * rate))
    cum_last = cum[:, L - 1 : L]
    to_end = jnp.exp(cum_last - cum)
    tw = to_end * step
    up = jnp.exp(cum)
    rows_s[0:8, :] = cum
    rows_s[8:16, :] = step
    rows_s[16:24, :] = tw
    rows_s[24:32, :] = up
    cols = jnp.transpose(rows_s[...])
    cols_s[...] = cols
    tw_e[...] = spread(cols, 16)
    up_e[...] = spread(cols, 24)
    st_e[...] = spread(cols, 8)
    decay_lanes = up_e[L - 1 : L, :]
    dec[...] = jnp.broadcast_to(decay_lanes, (8, INNER))

    b_val = xb[:, INNER : INNER + N]
    c_val = xb[:, INNER + N :]
    hi, lo = split(xb[:, :INNER].astype(F32) * tw_e[...])
    loc[0] = dot_tn(b_val, hi) + dot_tn(b_val, lo)
    hi, lo = split(cot_ref[...].astype(F32) * up_e[...])
    loc[1] = dot_tn(c_val, hi) + dot_tn(c_val, lo)

    @pl.when(z == 0)
    def _():
        rbuf[0] = jnp.zeros((NC, 2 * RC, INNER), F32)
        rfac[0] = jnp.ones((8, INNER), F32)

    @pl.when(z == NZ - 1)
    def _():
        rbuf[1] = jnp.zeros((NC, 2 * RC, INNER), F32)
        rfac[1] = jnp.ones((8, INNER), F32)

    pl.semaphore_wait(barrier, 2 + NX - 1 + 2 * NY - 1)

    first = (z >= NZ // 2).astype(jnp.int32)

    def nearer(way):
        return (place + 1 - 2 * way, dp)

    def hop(way, c):
        return pltpu.make_async_remote_copy(
            src_ref=sbuf.at[way, c],
            dst_ref=rbuf.at[way, c],
            send_sem=send_sem.at[way, c],
            recv_sem=recv_sem.at[way, c],
            device_id=nearer(way),
            device_id_type=MESH,
        )

    def factor_hop(way):
        return pltpu.make_async_remote_copy(
            src_ref=sfac.at[way],
            dst_ref=rfac.at[way],
            send_sem=fsend_sem.at[way],
            recv_sem=frecv_sem.at[way],
            device_id=nearer(way),
            device_id_type=MESH,
        )

    def has_in(way):
        return jnp.where(way == 0, z, NZ - 1 - z) > 0

    def has_out(way):
        return jnp.where(way == 0, NZ - 1 - z, z) > 0

    def relay_factor(way):
        @pl.when(has_in(way))
        def _():
            factor_hop(way).wait_recv()

        @pl.when(has_out(way))
        def _():
            sfac[way] = rfac[way] * dec[...]
            factor_hop(way).start()

    def relay(way, c):
        @pl.when(has_in(way))
        def _():
            hop(way, c).wait_recv()

        @pl.when(has_out(way))
        def _():
            rows = pl.ds(pl.multiple_of(c * RC, RC), RC)
            main = rbuf[way, c, 0:RC, :]
            aux = rbuf[way, c, RC : 2 * RC, :]
            sbuf[way, c, 0:RC, :] = dec[...] * main + loc[way, rows, :]
            sbuf[way, c, RC : 2 * RC, :] = aux + rfac[way] * loc[1 - way, rows, :]
            hop(way, c).start()

    def remote(src, dst, send, recv, target):
        return pltpu.make_async_remote_copy(
            src_ref=src, dst_ref=dst, send_sem=send, recv_sem=recv, device_id=target,
            device_id_type=MESH,
        )

    def across(k):
        return device(lax.rem(x + k, NX), y, ring, core)

    def exchange_factor():
        xfac[...] = rfac[0] * rfac[1] * dec[...]
        for k in range(1, NX):
            remote(xfac, xdec.at[x], xsend_sem.at[0, k], xrecv_sem.at[0, x], across(k)).start()

    def exchange(c):
        rows = pl.ds(pl.multiple_of(c * RC, RC), RC)
        xsend[0, c] = (
            rfac[1] * (dec[...] * rbuf[0, c, 0:RC, :] + loc[0, rows, :])
            + rbuf[1, c, RC : 2 * RC, :]
        )
        xsend[1, c] = (
            rfac[0] * (dec[...] * rbuf[1, c, 0:RC, :] + loc[1, rows, :])
            + rbuf[0, c, RC : 2 * RC, :]
        )
        for k in range(1, NX):
            kind = (lax.rem(x + k, NX) < x).astype(jnp.int32)
            remote(
                xsend.at[kind, c], xrecv.at[x, c], xsend_sem.at[1, k], xrecv_sem.at[1, x],
                across(k),
            ).start()

    def all_pieces(k, source):
        return remote(
            xrecv.at[source], xrecv.at[source], xsend_sem.at[1, k], xrecv_sem.at[1, source],
            across(k),
        )

    def the_factor(k, source):
        return remote(
            xfac, xdec.at[source], xsend_sem.at[0, k], xrecv_sem.at[0, source], across(k)
        )

    def relay_first(c, _):
        relay(first, c)
        return 0

    def relay_second(c, _):
        relay(1 - first, c)
        exchange(c)
        return 0

    early = jnp.logical_or(z < 4, z >= NZ - 4)

    @pl.when(early)
    def _():
        relay_factor(first)
        lax.fori_loop(0, NC, relay_first, 0)

    pair_s[...] = jnp.zeros_like(pair_s)
    low = iota((128, 128), 1) < P_SIZE
    for sb in range(2):
        t0 = 128 * sb
        wide = L - t0
        rs = slice(t0, t0 + 128)
        gram = dot_nt(xb[rs, INNER : INNER + N], xb[t0:, INNER + N :])
        mask = iota((128, wide), 1) >= iota((128, wide), 0)
        dgram = jnp.zeros((128, wide), F32)
        for j in range(2):
            cot_t = cot_ref[t0:, 128 * j : 128 * j + 128]
            v_t = xb[rs, 128 * j : 128 * j + 128]
            parts = []
            for i in range(2):
                h = 2 * j + i
                keep = low if i == 0 else jnp.logical_not(low)
                v_h = jnp.where(keep, v_t.astype(F32), 0.0).astype(BF16)
                gap = rows_s[h : h + 1, t0:] - cols_s[rs, h : h + 1]
                within = jnp.exp(jnp.where(mask, gap, -1e30))
                dmix = dot_nt(v_h, cot_t)
                hi, lo = split(gram * within)
                parts.append(dot(hi, cot_t) + dot(lo, cot_t))
                dw = dmix * within * cols_s[rs, 8 + h : 9 + h]
                dgram = dgram + dw
                pair_s[h : h + 1, t0:] += jnp.sum(dw * gram, axis=0, keepdims=True)
            ac[rs, 128 * j : 128 * j + 128] = jnp.where(low, parts[0], parts[1])
        hi, lo = split(dgram)
        c_t = xb[t0:, INNER + N :]
        b_s = xb[rs, INNER : INNER + N]
        gbl[rs, :] = dot(hi, c_t) + dot(lo, c_t)
        from_here = dot_tn(hi, b_s) + dot_tn(lo, b_s)
        if sb == 0:
            gcl[...] = from_here
        else:
            gcl[t0:, :] += from_here

    @pl.when(jnp.logical_not(early))
    def _():
        relay_factor(first)
        lax.fori_loop(0, NC, relay_first, 0)

    relay_factor(1 - first)
    exchange_factor()
    lax.fori_loop(0, NC, relay_second, 0)

    for k in range(1, NX):
        source = lax.rem(x + k, NX)
        the_factor(k, source).wait_recv()
        all_pieces(k, source).wait_recv()

    def gather(c, _):
        rows = pl.ds(pl.multiple_of(c * RC, RC), RC)
        s_in[rows, :] = jnp.zeros((RC, INNER), F32)
        g_after[rows, :] = jnp.zeros((RC, INNER), F32)
        for k in range(NX - 1):

            @pl.when(k < x)
            def _():
                s_in[rows, :] = xdec[k] * s_in[rows, :] + xrecv[k, c]

        for k in range(NX - 1, 0, -1):

            @pl.when(k > x)
            def _():
                g_after[rows, :] = xdec[k] * g_after[rows, :] + xrecv[k, c]

        s_in[rows, :] = rbuf[0, c, 0:RC, :] + rfac[0] * s_in[rows, :]
        g_after[rows, :] = rbuf[1, c, 0:RC, :] + rfac[1] * g_after[rows, :]
        return 0

    lax.fori_loop(0, NC, gather, 0)

    @pl.when(z == 0)
    def _():
        pl.semaphore_signal(
            edge_sem, inc=1, device_id=device(x, y, lax.rem(ring + ZR - 1, ZR), core),
            device_id_type=MESH,
        )
        pl.semaphore_wait(edge_sem, 1)
        for k in range(1, NZ // 2):
            pl.semaphore_signal(
                known_sem, inc=1, device_id=device(x, y, ring + k, core), device_id_type=MESH
            )

    @pl.when(z == NZ - 1)
    def _():
        pl.semaphore_signal(
            edge_sem, inc=1, device_id=device(x, y, lax.rem(ring + 1, ZR), core),
            device_id_type=MESH,
        )
        pl.semaphore_wait(edge_sem, 1)
        for k in range(1, NZ // 2):
            pl.semaphore_signal(
                known_sem, inc=1, device_id=device(x, y, ring - k, core), device_id_type=MESH
            )

    b_val = xb[:, INNER : INNER + N]
    c_val = xb[:, INNER + N :]
    s_hi, s_lo = split(s_in[...])
    g_hi, g_lo = split(g_after[...])
    state_back = dot(b_val, g_hi) + dot(b_val, g_lo)
    state_proj = dot(c_val, s_hi) + dot(c_val, s_lo)
    cot = cot_ref[...].astype(F32)
    vals = xb[:, :INNER].astype(F32)
    scaled = cot * up_e[...]
    hi, lo = split(scaled)
    grad_c = gcl[...] + dot_nt(hi, s_hi) + dot_nt(hi, s_lo) + dot_nt(lo, s_hi)
    hi, lo = split(vals * tw_e[...])
    grad_b = gbl[...] + dot_nt(hi, g_hi) + dot_nt(hi, g_lo) + dot_nt(lo, g_hi)
    local_step = head_sums(vals * ac[...])
    tail_grad = head_sums(vals * state_back)
    proj_term = head_sums(scaled * state_proj)
    skip_lanes = spread(jnp.broadcast_to(0.0, (8, 128)) + sum(
        jnp.where(iota((8, 128), 1) == h, skip_ref[h], 0.0) for h in range(H)
    ), 0)[0:1, :]
    grad_vals = st_e[...] * ac[...] + skip_lanes * cot + tw_e[...] * state_back

    step = rows_s[8:16, :]
    tw = rows_s[16:24, :]
    cum = rows_s[0:8, :]
    cum_last = cum[:, L - 1 : L]
    sel = head_rows(F32)
    skip_sum = jnp.sum(sel * jnp.sum(cot * vals, axis=0, keepdims=True), axis=1, keepdims=True)
    both = jnp.sum(
        sel * jnp.sum(s_in[...] * g_after[...], axis=0, keepdims=True), axis=1, keepdims=True
    )
    tail_term = tail_grad * tw
    extra = jnp.sum(tail_term, axis=1, keepdims=True) + jnp.exp(cum_last) * both
    grad_cum = pair_s[...] - step * local_step + proj_term - tail_term
    since = (iota((L, L), 0) >= iota((L, L), 1)).astype(F32).astype(BF16)
    grad_log = sum(dot(part, since) for part in split3(grad_cum)) + extra
    rows_s[32 : 32 + H, :] = dt_ref[...]
    dt_pre = rows_s[32:40, :] + head_column(dt_bias_ref)
    rate = -jnp.exp(head_column(a_log_ref))
    grad_step = local_step + tail_grad * jnp.exp(cum_last - cum) + rate * grad_log
    grad_pre = grad_step / (1.0 + jnp.exp(-dt_pre))
    gpre_ref[...] = grad_pre[0:H, :]
    alog_sum = rate * jnp.sum(grad_log * step, axis=1, keepdims=True)
    bias_sum = jnp.sum(grad_pre, axis=1, keepdims=True)

    gc_pad[0:8, :] = jnp.zeros((8, CH), F32)
    gc_pad[8 + L : 16 + L, :] = jnp.zeros((8, CH), F32)
    for lanes, value in (
        (slice(0, INNER), grad_vals),
        (slice(INNER, INNER + N), grad_b),
        (slice(INNER + N, CH), grad_c),
    ):
        low_value = value.astype(BF16).astype(F32)
        sig = sig_s[:, lanes]
        gc_pad[8 : 8 + L, lanes] = low_value * sig * (1.0 + pre_s[:, lanes] * (1.0 - sig))

    spill_out[...] = sum(w_ref[k : k + 1, :] * gc_pad[3 - k : 11 - k, :] for k in range(K))

    def spill(target):
        return remote(spill_out, spill_in, ssend_sem.at[0], srecv_sem.at[0], (target, dp))

    @pl.when(place > 0)
    def _():
        spill(place - 1).start()

    sums_ref[...] = jnp.zeros_like(sums_ref)
    for k in range(K + 1):
        term = gc_pad[8 : 8 + L, :]
        if k < K:
            term = term * xp[5 + k : 5 + k + L, :]
        total = jnp.sum(term, axis=0, keepdims=True)
        for j in range(4):
            sums_ref[4 * k + j] = total[:, 128 * j : 128 * j + 128]
    lane = iota((8, 128), 1)
    row = iota((8, 128), 0)
    small = (
        jnp.where(lane == row, bias_sum, 0.0)
        + jnp.where(lane == row + 8, alog_sum, 0.0)
        + jnp.where(lane == row + 16, skip_sum, 0.0)
    )
    small = jnp.where(row < H, small, 0.0)
    sums_ref[20] = jnp.sum(small, axis=0, keepdims=True)

    me = (x * NY + y) * 2 + core

    def in_plane(k):
        r = lax.rem(me + k, NR)
        return r, device(r // 8, lax.rem(r // 2, NY), ring, lax.rem(r, 2))

    def all_of(buf, stage):
        part = buf.at[pl.ds(0, NR - 1)]
        return remote(part, part, rsend_sem.at[stage], rrecv_sem.at[stage], in_plane(1)[1])

    def scatter(k, _):
        r, target = in_plane(k)
        remote(sums_ref.at[r], plane.at[me], rsend_sem.at[0], rrecv_sem.at[0], target).start()
        return 0

    lax.fori_loop(1, NR, scatter, 0)
    plane[pl.ds(me, 1)] = sums_ref[pl.ds(me, 1)]
    for r in range(0, L, 64):
        rows = sum(
            w_ref[k : k + 1, :] * gc_pad[11 - k + r : 11 - k + r + 64, :] for k in range(K)
        )
        gx_ref[r : r + 64, :] = rows.astype(BF16)
        if r + 64 == L:
            tail = rows[48:64, :]

    @pl.when(jnp.logical_and(z > 0, z < NZ - 1))
    def _():
        pl.semaphore_wait(known_sem, 1)

    all_of(plane, 0).wait_recv()
    mine = jnp.sum(plane[...], axis=0, keepdims=True)
    own[0:1] = mine

    def along(k, _):
        q = lax.rem(ring + k, ZR)
        remote(
            own.at[0], line.at[ring], rsend_sem.at[1], rrecv_sem.at[1], device(x, y, q, core)
        ).start()
        return 0

    lax.fori_loop(1, ZR, along, 0)
    line[pl.ds(ring, 1)] = mine

    @pl.when(place < NX * NZ - 1)
    def _():
        spill(place + 1).wait_recv()

    @pl.when(place == NX * NZ - 1)
    def _():
        spill_in[...] = jnp.zeros_like(spill_in)

    gx_ref[L - 16 : L, :] = jnp.concatenate(
        [tail[0:8, :], tail[8:16, :] + spill_in[...]], axis=0
    ).astype(BF16)

    all_of(line, 1).wait_recv()
    total = jnp.sum(line[...], axis=0, keepdims=True)
    own[1:2] = total
    totals[pl.ds(me, 1)] = total

    def spread_out(k, _):
        remote(
            own.at[1], totals.at[me], rsend_sem.at[2], rrecv_sem.at[2], in_plane(k)[1]
        ).start()
        return 0

    lax.fori_loop(1, NR, spread_out, 0)
    def drain(c, _):
        for way in range(2):

            @pl.when(has_out(way))
            def _():
                hop(way, c).wait_send()

        return 0

    lax.fori_loop(0, NC, drain, 0)
    for way in range(2):

        @pl.when(has_out(way))
        def _():
            factor_hop(way).wait_send()

    for k in range(1, NX):
        source = lax.rem(x + k, NX)
        the_factor(k, source).wait_send()
        all_pieces(k, source).wait_send()

    @pl.when(place > 0)
    def _():
        spill(place - 1).wait_send()

    for stage, buf in enumerate((plane, line)):
        all_of(buf, stage).wait_send()
    all_of(totals, 2).wait_recv()
    for k in range(K):
        for j in range(4):
            wg_ref[k : k + 1, 128 * j : 128 * j + 128] = totals[4 * k + j]
    for j in range(4):
        bg_ref[0:1, 128 * j : 128 * j + 128] = totals[16 + j]
    small_ref[...] = totals[20]
    all_of(totals, 2).wait_send()


def run_main(halo, raw, weight, bias, dt_t, dt_bias, a_log, d_skip, cot):
    vmem = pl.BlockSpec(memory_space=pltpu.VMEM)
    smem = pl.BlockSpec(memory_space=pltpu.SMEM)
    hbm = pl.BlockSpec(memory_space=pl.ANY)
    return pl.pallas_call(
        main_kernel,
        out_shape=(
            jax.ShapeDtypeStruct((L, CH), BF16),
            jax.ShapeDtypeStruct((H, L), F32),
            jax.ShapeDtypeStruct((K, CH), F32),
            jax.ShapeDtypeStruct((1, CH), F32),
            jax.ShapeDtypeStruct((1, 128), F32),
        ),
        in_specs=[smem] * 3 + [vmem] + [hbm] * 5,
        out_specs=(vmem,) * 5,
        scratch_shapes=[
            pltpu.VMEM((L, CH), BF16),
            pltpu.VMEM((K, CH), F32),
            pltpu.VMEM((1, CH), F32),
            pltpu.VMEM((H, L), F32),
            pltpu.VMEM((L, INNER), BF16),
            pltpu.SemaphoreType.DMA((5,)),
            pltpu.VMEM((8 + L, CH), F32),
            pltpu.VMEM((L, CH), F32),
            pltpu.VMEM((L, CH), F32),
            pltpu.VMEM((L, CH), BF16),
            pltpu.VMEM((128, L), F32),
            pltpu.VMEM((L, 128), F32),
            pltpu.VMEM((2, N, INNER), F32),
            pltpu.VMEM((8, INNER), F32),
            pltpu.VMEM((L, INNER), F32),
            pltpu.VMEM((L, INNER), F32),
            pltpu.VMEM((L, INNER), F32),
            pltpu.VMEM((L, INNER), F32),
            pltpu.VMEM((L, N), F32),
            pltpu.VMEM((L, N), F32),
            pltpu.VMEM((8, L), F32),
            pltpu.VMEM((16 + L, CH), F32),
            pltpu.VMEM((2, NC, 2 * RC, INNER), F32),
            pltpu.VMEM((2, NC, 2 * RC, INNER), F32),
            pltpu.VMEM((2, 8, INNER), F32),
            pltpu.VMEM((2, 8, INNER), F32),
            pltpu.VMEM((2, NC, RC, INNER), F32),
            pltpu.VMEM((NX, NC, RC, INNER), F32),
            pltpu.VMEM((8, INNER), F32),
            pltpu.VMEM((NX, 8, INNER), F32),
            pltpu.VMEM((N, INNER), F32),
            pltpu.VMEM((N, INNER), F32),
            pltpu.VMEM((8, CH), F32),
            pltpu.VMEM((8, CH), F32),
            pltpu.VMEM((NR, 1, 128), F32),
            pltpu.VMEM((NR, 1, 128), F32),
            pltpu.VMEM((ZR, 1, 128), F32),
            pltpu.VMEM((2, 1, 128), F32),
            pltpu.VMEM((NR, 1, 128), F32),
            pltpu.SemaphoreType.DMA((2, NC)),
            pltpu.SemaphoreType.DMA((2, NC)),
            pltpu.SemaphoreType.DMA((2,)),
            pltpu.SemaphoreType.DMA((2,)),
            pltpu.SemaphoreType.DMA((2, NX)),
            pltpu.SemaphoreType.DMA((2, NX)),
            pltpu.SemaphoreType.DMA((1,)),
            pltpu.SemaphoreType.DMA((1,)),
            pltpu.SemaphoreType.DMA((3,)),
            pltpu.SemaphoreType.DMA((3,)),
            pltpu.SemaphoreType.REGULAR,
            pltpu.SemaphoreType.REGULAR,
        ],
        compiler_params=pltpu.CompilerParams(
            collective_id=0, has_side_effects=True, vmem_limit_bytes=48 << 20
        ),
        name="slab",
    )(dt_bias, a_log, d_skip, halo, raw, weight, bias, dt_t, cot)


def shift(block, axis, distance):
    devices = range(lax.axis_size(axis))
    route = [(i - distance, i) for i in devices if i - distance in devices]
    return lax.ppermute(block, axis, route)


def on_device(xbc_raw, conv_weight, conv_bias, dt_raw, dt_bias, a_log, d_skip, grad_out):
    raw = xbc_raw[0]
    halo = shift(raw[L - 8 :], "ctx", 1)
    gx, gpre, weight_grad, bias_grad, small = run_main(
        halo, raw, conv_weight, conv_bias[None], dt_raw[0].T, dt_bias, a_log, d_skip, grad_out[0]
    )
    return (
        gx[None], gpre.T[None], weight_grad, bias_grad[0], small[0, 0:4], small[0, 8:12],
        small[0, 16:20],
    )


def solution(mesh):
    rows = P("dp", "ctx", None)
    return jax.shard_map(
        on_device,
        mesh=mesh,
        in_specs=(rows, P(), P(), rows, P(), P(), P(), rows),
        out_specs=(rows, rows, P(), P(), P(), P(), P()),
        check_vma=False,
    )
```

time: 160 us -> 130 us (0.81)
  the two profiles are of different devices: /device:TPU:2 before, /device:TPU:1 now
where the time goes in v2:
time: 130 us
  Pallas kernels  118 us (91%)
  local copies, waits for them, and re-layouts  6.31 us (5%)
  starting transfers between devices  4.49 us (3%)
    pallas_call x1, Pallas kernels, run_main(): pl.pallas_call(main_kernel, out_shape=(jax.ShapeDtypeStruct((L, CH), BF16...  118 us
    unnamed x20, local copies, waits for them, and re-layouts  5.02 us
    ppermute x1, starting transfers between devices, shift(): return lax.ppermute(block, axis, route)  4.49 us
  transfers between devices with their start and end apart: 1, of which 1 were waited for; matrix products, arithmetic and copies ran while one was open for 0% of the time, Pallas kernels for 0%

profile of v2, /device:TPU:1, one launch (start us, length us, event | category | flops | bytes accessed | tf_op | source)
XLA Modules:
  0.0 130.1 jit_solution(5375242575546477366)
XLA Ops:
  0.6 0.0 copy-start.2
  0.6 0.7 slice_bitcast_fusion
  1.3 0.0 copy-start.3
  1.3 4.5 %collective-permute-start = (bf16[8,512]{1,0:T(8,128)(2,1)S(1)}, bf16[8,512]{1,0:T(8,128)(2,1)S(1)}, u32[]{:S(2)}, u32[]{:S(2)}) collective-permute-start(bf16[8,512]{1,0:T(8,128)(2,1)S(1)} %slice_bitcast_fusion), channel_id=1, source_target_pairs={{0,16},{16,32},{32,48},{48,64},{64,80},{80,96},{96,112},{112,128},... | collective-permute-start | bytes 24584 | tf_op jit(solution)/shard_map/ppermute | solution.py:666
  5.8 0.8 collective-permute-done.halo_ref
  6.6 0.0 copy-start.4
  6.6 0.0 copy-start.5
  6.6 0.0 copy-start.6
  6.6 0.0 copy-start.7
  6.6 0.0 copy-done.2
  6.6 0.0 copy-done.3
  6.6 0.7 copy-done.4
  7.3 0.0 copy-done.5
  7.3 0.0 copy-done.6
  7.3 0.0 copy-done.7
  7.3 0.0 copy-start
  7.3 0.9 copy-done
  8.3 0.0 copy-start.1
  8.3 0.9 copy-done.1
  9.2 117.9 %slab.1 = (bf16[256,512]{1,0:T(8,128)(2,1)S(1)}, f32[4,256]{1,0:T(4,128)S(1)}, f32[4,512]{1,0:T(4,128)S(1)}, f32[1,512]{1,0:T(1,128)S(1)}, f32[1,128]{1,0:T(1,128)S(1)}) custom-call(f32[4]{0:T(128)S(1)} %copy-done.5, f32[4]{0:T(128)S(1)} %copy-done.6, f32[4]{0:T(128)S(1)} %copy-done.7, bf16[8,512]{1,0:T(8,128)(2,1)S(1)} %collective-permute-done.halo_ref, ...), custom_call_target="tpu_custom_call" | custom-call | tf_op jit(solution)/shard_map/slab/pallas_call | solution.py:592
  127.1 0.6 slice_bitcast_fusion.1
  127.7 0.7 copy.19
  128.4 0.6 copy.20
  129.0 0.6 copy.21
  129.6 0.6 copy.22
Async XLA Ops:
  0.6 6.0 %copy-start.2 = (f32[4,512]{1,0:T(4,128)S(1)}, f32[4,512]{1,0:T(4,128)}, u32[]{:S(2)}) copy-start(f32[4,512]{1,0:T(4,128)} %w_hbm.1) | copy-start | bytes 24580
  1.3 5.3 %copy-start.3 = (f32[1,256,4]{1,2,0:T(4,128)S(1)}, f32[1,256,4]{1,2,0:T(4,128)}, u32[]{:S(2)}) copy-start(f32[1,256,4]{1,2,0:T(4,128)} %param.11) | copy-start | bytes 12292
  1.3 5.3 %collective-permute-start = (bf16[8,512]{1,0:T(8,128)(2,1)S(1)}, bf16[8,512]{1,0:T(8,128)(2,1)S(1)}, u32[]{:S(2)}, u32[]{:S(2)}) collective-permute-start(bf16[8,512]{1,0:T(8,128)(2,1)S(1)} %slice_bitcast_fusion), channel_id=1, source_target_pairs={{0,16},{16,32},{32,48},{48,64},{64,80},{80,96},{96,112},{112,128},... | collective-permute-start | bytes 24584 | tf_op jit(solution)/shard_map/ppermute | solution.py:666
  6.6 0.7 copy-start.4
  6.6 0.7 copy-start.5
  6.6 0.7 copy-start.6
  6.6 0.7 copy-start.7
  7.3 0.9 copy-start
  8.3 0.9 copy-start.1

commit v3 on v2

v3 whole, which is shorter than its diff:
```python
import functools

import jax
import jax.numpy as jnp
from jax import lax
from jax.experimental import pallas as pl
from jax.experimental.pallas import tpu as pltpu
from jax.sharding import PartitionSpec as P

H = 4
P_SIZE = 64
N = 128
K = 4
L = 256
CH = 512
INNER = H * P_SIZE
NZ = 16
NX = 4
NY = 4
NR = 32
ZR = 32
NB = 4
NO = 16
RC = N // NO
F32 = jnp.float32
BF16 = jnp.bfloat16
MESH = pl.DeviceIdType.MESH


def dot(a, b):
    return lax.dot_general(a, b, (((1,), (0,)), ((), ())), preferred_element_type=F32)


def dot_nt(a, b):
    return lax.dot_general(a, b, (((1,), (1,)), ((), ())), preferred_element_type=F32)


def dot_tn(a, b):
    return lax.dot_general(a, b, (((0,), (0,)), ((), ())), preferred_element_type=F32)


def split(a):
    hi = a.astype(BF16)
    return hi, (a - hi.astype(F32)).astype(BF16)


def split3(a):
    hi = a.astype(BF16)
    rest = a - hi.astype(F32)
    mid = rest.astype(BF16)
    return hi, mid, (rest - mid.astype(F32)).astype(BF16)


def iota(shape, dim):
    return lax.broadcasted_iota(jnp.int32, shape, dim)


def head_column(ref):
    rows = iota((8, 1), 0)
    col = jnp.zeros((8, 1), F32)
    for h in range(H):
        col = jnp.where(rows == h, ref[h], col)
    return col


def spread(cols, first):
    rows = cols.shape[0]
    low = iota((rows, 128), 1) < P_SIZE
    tiles = []
    for j in range(2):
        a = jnp.broadcast_to(cols[:, first + 2 * j : first + 2 * j + 1], (rows, 128))
        b = jnp.broadcast_to(cols[:, first + 2 * j + 1 : first + 2 * j + 2], (rows, 128))
        tiles.append(jnp.where(low, a, b))
    return jnp.concatenate(tiles, axis=1)


def head_rows(dtype):
    return (iota((8, INNER), 1) // P_SIZE == iota((8, INNER), 0)).astype(dtype)


def head_sums(x):
    sel = head_rows(F32).astype(BF16)
    hi, lo = split(x)
    return dot_nt(sel, hi) + dot_nt(sel, lo)


def main_kernel(
    dt_bias_ref, a_log_ref, skip_ref, raw_hbm, w_hbm, bias_hbm, dt_hbm, cot_hbm,
    gx_ref, gpre_ref, wg_ref, bg_ref, small_ref,
    raw_ref, w_ref, bias_ref, dt_ref, cot_ref, in_sem,
    xp, pre_s, sig_s, xb, rows_s, cols_s, loc, dec, tw_e, up_e, st_e, ac, gbl, gcl, pair_s,
    gc_pad, abuf, dbuf, pre_p, pre_q, tot, blk, rbuf, sbuf, rfac, sfac, heads, tails, cfull, corr,
    rsend, ret, near_out, near_in, spill_out, spill_in, sums_ref, plane, line, own, totals,
    send_sem, recv_sem, fsend_sem, frecv_sem, asend_sem, arecv_sem, hsend_sem, hrecv_sem,
    hcast_sem, nsend_sem, nrecv_sem, ssend_sem, srecv_sem, rsend_sem, rrecv_sem, edge_sem,
    known_sem,
):
    place = lax.axis_index("ctx")
    dp = lax.axis_index("dp")
    z = lax.rem(place, NZ)
    x = place // NZ
    y = dp // 4
    z_hi = lax.rem(dp // 2, 2)
    core = lax.rem(dp, 2)

    def device(x_, y_, ring, core_):
        return (x_ * NZ + lax.rem(ring, NZ), y_ * 4 + (ring // NZ) * 2 + core_)

    ring = z_hi * NZ + z
    zq = z // NB
    zi = lax.rem(z, NB)
    me_o = x * NB + zi

    def remote(src, dst, send, recv, target):
        return pltpu.make_async_remote_copy(
            src_ref=src, dst_ref=dst, send_sem=send, recv_sem=recv, device_id=target,
            device_id_type=MESH,
        )

    def mate(k):
        o = lax.rem(me_o + k, NO)
        return o, ((o // NB) * NZ + zq * NB + lax.rem(o, NB), dp)

    heads[...] = jnp.zeros_like(heads)
    tails[...] = jnp.zeros_like(tails)
    barrier = pltpu.get_barrier_semaphore()
    inputs = [
        pltpu.make_async_copy(src, dst, in_sem.at[i])
        for i, (src, dst) in enumerate(
            ((raw_hbm, raw_ref), (w_hbm, w_ref), (bias_hbm, bias_ref), (dt_hbm, dt_ref),
             (cot_hbm, cot_ref))
        )
    ]
    for copy in inputs:
        copy.start()
    for step in (1, ZR - 1, NB, ZR - NB):
        pl.semaphore_signal(
            barrier, inc=1, device_id=device(x, y, lax.rem(ring + step, ZR), core),
            device_id_type=MESH,
        )

    def greet(k, _):
        pl.semaphore_signal(barrier, inc=1, device_id=mate(k)[1], device_id_type=MESH)
        return 0

    lax.fori_loop(1, NO, greet, 0)
    for k in range(1, 2 * NY):
        q = lax.rem(y * 2 + core + k, 2 * NY)
        pl.semaphore_signal(
            barrier, inc=1, device_id=device(x, q // 2, ring, lax.rem(q, 2)), device_id_type=MESH
        )
    for copy in inputs:
        copy.wait()

    xp[0:8, :] = jnp.zeros((8, CH), F32)
    xp[8 : 8 + L, :] = raw_ref[...].astype(F32)

    def activate(r, size):
        pre = bias_ref[...] + sum(
            w_ref[k : k + 1, :] * xp[5 + k + r : 5 + k + r + size, :] for k in range(K)
        )
        sig = 1.0 / (1.0 + jnp.exp(-pre))
        pre_s[r : r + size, :] = pre
        sig_s[r : r + size, :] = sig
        xb[r : r + size, :] = (pre * sig).astype(BF16)

    for r in range(0, L, 64):
        activate(r, 64)

    rate = -jnp.exp(head_column(a_log_ref))
    live = iota((8, 1), 0) < H
    rate = jnp.where(live, rate, 0.0)
    rows_s[...] = jnp.zeros_like(rows_s)
    rows_s[0:H, :] = dt_ref[...]
    dt_pre = rows_s[0:8, :] + head_column(dt_bias_ref)
    step = jnp.where(
        live, jnp.maximum(dt_pre, 0.0) + jnp.log1p(jnp.exp(-jnp.abs(dt_pre))), 0.0
    )
    upto = (iota((L, L), 0) <= iota((L, L), 1)).astype(F32).astype(BF16)
    cum = sum(dot(part, upto) for part in split3(step * rate))
    cum_last = cum[:, L - 1 : L]
    to_end = jnp.exp(cum_last - cum)
    tw = to_end * step
    up = jnp.exp(cum)
    rows_s[0:8, :] = cum
    rows_s[8:16, :] = step
    rows_s[16:24, :] = tw
    rows_s[24:32, :] = up
    cols = jnp.transpose(rows_s[...])
    cols_s[...] = cols
    tw_e[...] = spread(cols, 16)
    up_e[...] = spread(cols, 24)
    st_e[...] = spread(cols, 8)
    dec[0] = up_e[L - 1 : L, :]
    near_out[0:3, :] = xp[5 + L : 8 + L, :]

    pl.semaphore_wait(barrier, 4 + NO - 1 + 2 * NY - 1)

    def near(target):
        return remote(
            near_out.at[0:3], near_in.at[0:3], nsend_sem.at[0], nrecv_sem.at[0], (target, dp)
        )

    @pl.when(z < NZ - 1)
    def _():
        near(place + 1).start()

    def head(l, send, target):
        return remote(heads.at[l, 0:3], heads.at[l, 0:3], send, hrecv_sem.at[0, l], target)

    def last(l, send, target):
        return remote(tails.at[l, 0:3], tails.at[l, 0:3], send, hrecv_sem.at[1, l], target)

    @pl.when(z == 0)
    def _():
        heads[x, 0:3, 0:CH] = pre_s[0:3, :]
        heads[x, 0:3, CH : CH + INNER] = tw_e[0:3, :]
        heads[x, 0:3, CH + INNER :] = (cot_ref[...].astype(F32) * up_e[...])[0:3, :]

        def cast(k, _):
            o, target = mate(k)
            head(x, hcast_sem.at[k], target).start()
            return 0

        lax.fori_loop(1, NO, cast, 0)

    has_tail = jnp.logical_and(z == NZ - 1, x < NX - 1)

    @pl.when(has_tail)
    def _():
        tails[x + 1, 0:3, :] = near_out[0:3, :]

        def cast(k, _):
            o, target = mate(k)
            last(x + 1, hcast_sem.at[k], target).start()
            return 0

        lax.fori_loop(1, NO, cast, 0)

    @pl.when(z > 0)
    def _():
        near(place - 1).wait_recv()
        xp[5:8, :] = near_in[0:3, :]
        activate(0, 16)

    ready = jnp.logical_or(iota((L, INNER), 0) >= 3, z > 0)
    b_val = xb[:, INNER : INNER + N]
    c_val = xb[:, INNER + N :]
    hi, lo = split(jnp.where(ready, xb[:, :INNER].astype(F32) * tw_e[...], 0.0))
    loc[:, 0:RC, :] = (dot_tn(b_val, hi) + dot_tn(b_val, lo)).reshape(NO, RC, INNER)
    hi, lo = split(jnp.where(ready, cot_ref[...].astype(F32) * up_e[...], 0.0))
    loc[:, RC:, :] = (dot_tn(c_val, hi) + dot_tn(c_val, lo)).reshape(NO, RC, INNER)

    def to_owners(k, _):
        o, target = mate(k)
        remote(dec.at[0], dbuf.at[me_o], asend_sem.at[0], arecv_sem.at[0], target).start()
        remote(loc.at[o], abuf.at[me_o], asend_sem.at[1], arecv_sem.at[1], target).start()
        return 0

    lax.fori_loop(1, NO, to_owners, 0)
    abuf[pl.ds(me_o, 1)] = loc[pl.ds(me_o, 1)]
    dbuf[pl.ds(me_o, 1)] = dec[...]

    def from_block(buf, i):
        part = buf.at[pl.ds(0, NO - 1)]
        return remote(part, part, asend_sem.at[i], arecv_sem.at[i], mate(1)[1])

    def along_line(step):
        return (place + NB * step, dp)

    def relay_heads():
        for l in range(NX):

            @pl.when(jnp.logical_not(jnp.logical_and(z == 0, x == l)))
            def _():
                head(l, hsend_sem.at[0, l], along_line(1)).wait_recv()

            @pl.when(zq < NB - 1)
            def _():
                head(l, hsend_sem.at[0, l], along_line(1)).start()

    def relay_tails():
        for l in range(1, NX):

            @pl.when(jnp.logical_not(jnp.logical_and(z == NZ - 1, x == l - 1)))
            def _():
                last(l, hsend_sem.at[1, l], along_line(-1)).wait_recv()

            @pl.when(zq > 0)
            def _():
                last(l, hsend_sem.at[1, l], along_line(-1)).start()

    def local_terms():
        pair_s[...] = jnp.zeros_like(pair_s)
        low = iota((128, 128), 1) < P_SIZE
        for sb in range(2):
            t0 = 128 * sb
            wide = L - t0
            rs = slice(t0, t0 + 128)
            gram = dot_nt(xb[rs, INNER : INNER + N], xb[t0:, INNER + N :])
            mask = iota((128, wide), 1) >= iota((128, wide), 0)
            dgram = jnp.zeros((128, wide), F32)
            for j in range(2):
                cot_t = cot_ref[t0:, 128 * j : 128 * j + 128]
                v_t = xb[rs, 128 * j : 128 * j + 128]
                parts = []
                for i in range(2):
                    h = 2 * j + i
                    keep = low if i == 0 else jnp.logical_not(low)
                    v_h = jnp.where(keep, v_t.astype(F32), 0.0).astype(BF16)
                    gap = rows_s[h : h + 1, t0:] - cols_s[rs, h : h + 1]
                    within = jnp.exp(jnp.where(mask, gap, -1e30))
                    dmix = dot_nt(v_h, cot_t)
                    hi, lo = split(gram * within)
                    parts.append(dot(hi, cot_t) + dot(lo, cot_t))
                    dw = dmix * within * cols_s[rs, 8 + h : 9 + h]
                    dgram = dgram + dw
                    pair_s[h : h + 1, t0:] += jnp.sum(dw * gram, axis=0, keepdims=True)
                ac[rs, 128 * j : 128 * j + 128] = jnp.where(low, parts[0], parts[1])
            hi, lo = split(dgram)
            c_t = xb[t0:, INNER + N :]
            b_s = xb[rs, INNER : INNER + N]
            gbl[rs, :] = dot(hi, c_t) + dot(lo, c_t)
            from_here = dot_tn(hi, b_s) + dot_tn(lo, b_s)
            if sb == 0:
                gcl[...] = from_here
            else:
                gcl[t0:, :] += from_here

    @pl.when(z > 0)
    def _():
        local_terms()

    left = zq < NB // 2

    @pl.when(left)
    def _():
        relay_heads()

    @pl.when(jnp.logical_not(left))
    def _():
        relay_tails()

    from_block(dbuf, 0).wait_recv()
    from_block(abuf, 1).wait_recv()
    for l in range(NX):
        p = abuf[NB * l, 0:RC, :]
        q = abuf[NB * l + NB - 1, RC:, :]
        for i in range(1, NB):
            pre_p[NB * l + i] = p
            p = dbuf[NB * l + i] * p + abuf[NB * l + i, 0:RC, :]
            j = NB - 1 - i
            pre_q[NB * l + j] = q
            q = dbuf[NB * l + j] * q + abuf[NB * l + j, RC:, :]
        tot[0, l] = p
        tot[1, l] = q
        blk[l] = dbuf[NB * l] * dbuf[NB * l + 1] * dbuf[NB * l + 2] * dbuf[NB * l + 3]

    @pl.when(zq == 0)
    def _():
        rbuf[0] = jnp.zeros((NX, 2 * RC, INNER), F32)
        rfac[0] = jnp.ones((8, INNER), F32)

    @pl.when(zq == NB - 1)
    def _():
        rbuf[1] = jnp.zeros((NX, 2 * RC, INNER), F32)
        rfac[1] = jnp.ones((8, INNER), F32)

    first = jnp.where(left, 0, 1)

    def hop(way, l):
        return remote(
            sbuf.at[way, l], rbuf.at[way, l], send_sem.at[way, l], recv_sem.at[way, l],
            along_line(1 - 2 * way),
        )

    def factor_hop(way):
        return remote(
            sfac.at[way], rfac.at[way], fsend_sem.at[way], frecv_sem.at[way],
            along_line(1 - 2 * way),
        )

    def has_in(way):
        return jnp.where(way == 0, zq, NB - 1 - zq) > 0

    def has_out(way):
        return jnp.where(way == 0, NB - 1 - zq, zq) > 0

    def head_weights(l):
        v0 = jnp.where(zq == 0, 0.0, rfac[0, 4 + l : 5 + l, :])
        v1 = jnp.where(zq == 0, 1.0, v0 * dbuf[NB * l])
        v2 = v1 * dbuf[NB * l + 1]
        v3 = v2 * dbuf[NB * l + 2]
        return v0, v1, v2, v3, v3 * dbuf[NB * l + 3]

    def relay(way):
        @pl.when(has_in(way))
        def _():
            factor_hop(way).wait_recv()

        @pl.when(has_out(way))
        def _():
            for l in range(NX):
                sfac[way, l : l + 1, :] = rfac[way, l : l + 1, :] * blk[l]
                sfac[way, 4 + l : 5 + l, :] = (
                    head_weights(l)[4] if way == 0 else jnp.zeros((1, INNER), F32)
                )
            factor_hop(way).start()

        for l in range(NX):

            @pl.when(has_in(way))
            def _():
                hop(way, l).wait_recv()

            @pl.when(has_out(way))
            def _():
                sbuf[way, l, 0:RC, :] = blk[l] * rbuf[way, l, 0:RC, :] + tot[way, l]
                sbuf[way, l, RC:, :] = (
                    rbuf[way, l, RC:, :] + rfac[way, l : l + 1, :] * tot[1 - way, l]
                )
                hop(way, l).start()

    @pl.when(left)
    def _():
        relay(0)
        relay_tails()

    @pl.when(jnp.logical_not(left))
    def _():
        relay(1)
        relay_heads()

    @pl.when(z == 0)
    def _():
        xp[5:8, :] = tails[x, 0:3, :]
        activate(0, 16)
        local_terms()

    mine_rows = pl.ds(pl.multiple_of(me_o * RC, RC), RC)
    for l in range(NX):
        pre = heads[l, :, 0:CH] + sum(w_ref[k : k + 1, :] * tails[l, k : k + 8, :] for k in range(3))
        act = jnp.where(iota((8, CH), 0) < 3, pre / (1.0 + jnp.exp(-pre)), 0.0).astype(BF16)
        hi, lo = split(act[:, :INNER].astype(F32) * heads[l, :, CH : CH + INNER])
        b_row = act[:, INNER : INNER + N]
        c_row = act[:, INNER + N :]
        cfull[...] = dot_tn(b_row, hi) + dot_tn(b_row, lo)
        corr[0, l] = cfull[mine_rows, :]
        hi, lo = split(heads[l, :, CH + INNER :])
        cfull[...] = dot_tn(c_row, hi) + dot_tn(c_row, lo)
        corr[1, l] = cfull[mine_rows, :]

    @pl.when(left)
    def _():
        relay(1)

    @pl.when(jnp.logical_not(left))
    def _():
        relay(0)

    def line_terms(l):
        f = rfac[0, l : l + 1, :]
        e = rfac[1, l : l + 1, :]
        return f, e, f * e * blk[l]

    def give_back(l, i, entering, way):
        rsend[NB * l + i, RC * way : RC * way + RC, :] = entering

    carry = jnp.zeros((RC, INNER), F32)
    for l in range(NX):
        f, e, whole = line_terms(l)
        weights = head_weights(l)
        at = rbuf[0, l, 0:RC, :] + f * carry
        for i in range(NB):
            here = at + weights[i] * corr[0, l]
            if i:
                here = here + pre_p[NB * l + i]
            give_back(l, i, here, 0)
            at = at * dbuf[NB * l + i]
        total = (
            e * (blk[l] * rbuf[0, l, 0:RC, :] + tot[0, l] + weights[4] * corr[0, l])
            + rbuf[1, l, RC:, :]
        )
        carry = whole * carry + total
    carry = jnp.zeros((RC, INNER), F32)
    for l in range(NX - 1, -1, -1):
        f, e, whole = line_terms(l)
        at = rbuf[1, l, 0:RC, :] + e * carry
        for i in range(NB - 1, -1, -1):
            here = at
            if i < NB - 1:
                here = here + pre_q[NB * l + i]
            give_back(l, i, here, 1)
            at = at * dbuf[NB * l + i]
        total = (
            f * (blk[l] * rbuf[1, l, 0:RC, :] + tot[1, l]) + rbuf[0, l, RC:, :] + corr[1, l]
        )
        carry = whole * carry + total

    def back(k, _):
        o, target = mate(k)
        remote(rsend.at[o], ret.at[me_o], asend_sem.at[2], arecv_sem.at[2], target).start()
        return 0

    lax.fori_loop(1, NO, back, 0)
    ret[pl.ds(me_o, 1)] = rsend[pl.ds(me_o, 1)]

    @pl.when(zq == 0)
    def _():
        pl.semaphore_signal(
            edge_sem, inc=1, device_id=device(x, y, lax.rem(ring + ZR - NB, ZR), core),
            device_id_type=MESH,
        )
        pl.semaphore_wait(edge_sem, 1)
        pl.semaphore_signal(known_sem, inc=1, device_id=along_line(1), device_id_type=MESH)

    @pl.when(zq == NB - 1)
    def _():
        pl.semaphore_signal(
            edge_sem, inc=1, device_id=device(x, y, lax.rem(ring + NB, ZR), core),
            device_id_type=MESH,
        )
        pl.semaphore_wait(edge_sem, 1)
        pl.semaphore_signal(known_sem, inc=1, device_id=along_line(-1), device_id_type=MESH)

    from_block(ret, 2).wait_recv()
    s_in = ret[:, 0:RC, :].reshape(N, INNER)
    g_after = ret[:, RC:, :].reshape(N, INNER)

    b_val = xb[:, INNER : INNER + N]
    c_val = xb[:, INNER + N :]
    s_hi, s_lo = split(s_in)
    g_hi, g_lo = split(g_after)
    state_back = dot(b_val, g_hi) + dot(b_val, g_lo)
    state_proj = dot(c_val, s_hi) + dot(c_val, s_lo)
    cot = cot_ref[...].astype(F32)
    vals = xb[:, :INNER].astype(F32)
    scaled = cot * up_e[...]
    hi, lo = split(scaled)
    grad_c = gcl[...] + dot_nt(hi, s_hi) + dot_nt(hi, s_lo) + dot_nt(lo, s_hi)
    hi, lo = split(vals * tw_e[...])
    grad_b = gbl[...] + dot_nt(hi, g_hi) + dot_nt(hi, g_lo) + dot_nt(lo, g_hi)
    local_step = head_sums(vals * ac[...])
    tail_grad = head_sums(vals * state_back)
    proj_term = head_sums(scaled * state_proj)
    skip_lanes = spread(jnp.broadcast_to(0.0, (8, 128)) + sum(
        jnp.where(iota((8, 128), 1) == h, skip_ref[h], 0.0) for h in range(H)
    ), 0)[0:1, :]
    grad_vals = st_e[...] * ac[...] + skip_lanes * cot + tw_e[...] * state_back

    step = rows_s[8:16, :]
    tw = rows_s[16:24, :]
    cum = rows_s[0:8, :]
    cum_last = cum[:, L - 1 : L]
    sel = head_rows(F32)
    skip_sum = jnp.sum(sel * jnp.sum(cot * vals, axis=0, keepdims=True), axis=1, keepdims=True)
    both = jnp.sum(
        sel * jnp.sum(s_in * g_after, axis=0, keepdims=True), axis=1, keepdims=True
    )
    tail_term = tail_grad * tw
    extra = jnp.sum(tail_term, axis=1, keepdims=True) + jnp.exp(cum_last) * both
    grad_cum = pair_s[...] - step * local_step + proj_term - tail_term
    since = (iota((L, L), 0) >= iota((L, L), 1)).astype(F32).astype(BF16)
    grad_log = sum(dot(part, since) for part in split3(grad_cum)) + extra
    rows_s[32 : 32 + H, :] = dt_ref[...]
    dt_pre = rows_s[32:40, :] + head_column(dt_bias_ref)
    rate = -jnp.exp(head_column(a_log_ref))
    grad_step = local_step + tail_grad * jnp.exp(cum_last - cum) + rate * grad_log
    grad_pre = grad_step / (1.0 + jnp.exp(-dt_pre))
    gpre_ref[...] = grad_pre[0:H, :]
    alog_sum = rate * jnp.sum(grad_log * step, axis=1, keepdims=True)
    bias_sum = jnp.sum(grad_pre, axis=1, keepdims=True)

    gc_pad[0:8, :] = jnp.zeros((8, CH), F32)
    gc_pad[8 + L : 16 + L, :] = jnp.zeros((8, CH), F32)
    for lanes, value in (
        (slice(0, INNER), grad_vals),
        (slice(INNER, INNER + N), grad_b),
        (slice(INNER + N, CH), grad_c),
    ):
        low_value = value.astype(BF16).astype(F32)
        sig = sig_s[:, lanes]
        gc_pad[8 : 8 + L, lanes] = low_value * sig * (1.0 + pre_s[:, lanes] * (1.0 - sig))

    spill_out[...] = sum(w_ref[k : k + 1, :] * gc_pad[3 - k : 11 - k, :] for k in range(K))

    def spill(target):
        return remote(spill_out, spill_in, ssend_sem.at[0], srecv_sem.at[0], (target, dp))

    @pl.when(place > 0)
    def _():
        spill(place - 1).start()

    sums_ref[...] = jnp.zeros_like(sums_ref)
    for k in range(K + 1):
        term = gc_pad[8 : 8 + L, :]
        if k < K:
            term = term * xp[5 + k : 5 + k + L, :]
        total = jnp.sum(term, axis=0, keepdims=True)
        for j in range(4):
            sums_ref[4 * k + j] = total[:, 128 * j : 128 * j + 128]
    lane = iota((8, 128), 1)
    row = iota((8, 128), 0)
    small = (
        jnp.where(lane == row, bias_sum, 0.0)
        + jnp.where(lane == row + 8, alog_sum, 0.0)
        + jnp.where(lane == row + 16, skip_sum, 0.0)
    )
    small = jnp.where(row < H, small, 0.0)
    sums_ref[20] = jnp.sum(small, axis=0, keepdims=True)

    me = (x * NY + y) * 2 + core

    def in_plane(k):
        r = lax.rem(me + k, NR)
        return r, device(r // 8, lax.rem(r // 2, NY), ring, lax.rem(r, 2))

    def all_of(buf, stage):
        part = buf.at[pl.ds(0, NR - 1)]
        return remote(part, part, rsend_sem.at[stage], rrecv_sem.at[stage], in_plane(1)[1])

    def scatter(k, _):
        r, target = in_plane(k)
        remote(sums_ref.at[r], plane.at[me], rsend_sem.at[0], rrecv_sem.at[0], target).start()
        return 0

    lax.fori_loop(1, NR, scatter, 0)
    plane[pl.ds(me, 1)] = sums_ref[pl.ds(me, 1)]
    for r in range(0, L, 64):
        rows = sum(
            w_ref[k : k + 1, :] * gc_pad[11 - k + r : 11 - k + r + 64, :] for k in range(K)
        )
        gx_ref[r : r + 64, :] = rows.astype(BF16)
        if r + 64 == L:
            tail = rows[48:64, :]

    @pl.when(jnp.logical_and(zq > 0, zq < NB - 1))
    def _():
        pl.semaphore_wait(known_sem, 1)

    all_of(plane, 0).wait_recv()
    mine = jnp.sum(plane[...], axis=0, keepdims=True)
    own[0:1] = mine

    def along(k, _):
        q = lax.rem(ring + k, ZR)
        remote(
            own.at[0], line.at[ring], rsend_sem.at[1], rrecv_sem.at[1], device(x, y, q, core)
        ).start()
        return 0

    lax.fori_loop(1, ZR, along, 0)
    line[pl.ds(ring, 1)] = mine

    @pl.when(place < NX * NZ - 1)
    def _():
        spill(place + 1).wait_recv()

    @pl.when(place == NX * NZ - 1)
    def _():
        spill_in[...] = jnp.zeros_like(spill_in)

    gx_ref[L - 16 : L, :] = jnp.concatenate(
        [tail[0:8, :], tail[8:16, :] + spill_in[...]], axis=0
    ).astype(BF16)

    all_of(line, 1).wait_recv()
    total = jnp.sum(line[...], axis=0, keepdims=True)
    own[1:2] = total
    totals[pl.ds(me, 1)] = total

    def spread_out(k, _):
        remote(
            own.at[1], totals.at[me], rsend_sem.at[2], rrecv_sem.at[2], in_plane(k)[1]
        ).start()
        return 0

    lax.fori_loop(1, NR, spread_out, 0)
    for way in range(2):

        @pl.when(has_out(way))
        def _():
            factor_hop(way).wait_send()
            for l in range(NX):
                hop(way, l).wait_send()

    @pl.when(zq < NB - 1)
    def _():
        for l in range(NX):
            head(l, hsend_sem.at[0, l], along_line(1)).wait_send()

    @pl.when(zq > 0)
    def _():
        for l in range(1, NX):
            last(l, hsend_sem.at[1, l], along_line(-1)).wait_send()

    @pl.when(z == 0)
    def _():
        for k in range(1, NO):
            head(0, hcast_sem.at[k], along_line(1)).wait_send()

    @pl.when(has_tail)
    def _():
        for k in range(1, NO):
            last(0, hcast_sem.at[k], along_line(-1)).wait_send()

    @pl.when(z < NZ - 1)
    def _():
        near(place + 1).wait_send()

    for i, buf in enumerate((dbuf, abuf, ret)):
        from_block(buf, i).wait_send()

    @pl.when(place > 0)
    def _():
        spill(place - 1).wait_send()

    for stage, buf in enumerate((plane, line)):
        all_of(buf, stage).wait_send()
    all_of(totals, 2).wait_recv()
    for k in range(K):
        for j in range(4):
            wg_ref[k : k + 1, 128 * j : 128 * j + 128] = totals[4 * k + j]
    for j in range(4):
        bg_ref[0:1, 128 * j : 128 * j + 128] = totals[16 + j]
    small_ref[...] = totals[20]
    all_of(totals, 2).wait_send()


def run_main(raw, weight, bias, dt_t, dt_bias, a_log, d_skip, cot):
    vmem = pl.BlockSpec(memory_space=pltpu.VMEM)
    smem = pl.BlockSpec(memory_space=pltpu.SMEM)
    hbm = pl.BlockSpec(memory_space=pl.ANY)
    return pl.pallas_call(
        main_kernel,
        out_shape=(
            jax.ShapeDtypeStruct((L, CH), BF16),
            jax.ShapeDtypeStruct((H, L), F32),
            jax.ShapeDtypeStruct((K, CH), F32),
            jax.ShapeDtypeStruct((1, CH), F32),
            jax.ShapeDtypeStruct((1, 128), F32),
        ),
        in_specs=[smem] * 3 + [hbm] * 5,
        out_specs=(vmem,) * 5,
        scratch_shapes=[
            pltpu.VMEM((L, CH), BF16),
            pltpu.VMEM((K, CH), F32),
            pltpu.VMEM((1, CH), F32),
            pltpu.VMEM((H, L), F32),
            pltpu.VMEM((L, INNER), BF16),
            pltpu.SemaphoreType.DMA((5,)),
            pltpu.VMEM((8 + L, CH), F32),
            pltpu.VMEM((L, CH), F32),
            pltpu.VMEM((L, CH), F32),
            pltpu.VMEM((L, CH), BF16),
            pltpu.VMEM((128, L), F32),
            pltpu.VMEM((L, 128), F32),
            pltpu.VMEM((NO, 2 * RC, INNER), F32),
            pltpu.VMEM((1, 1, INNER), F32),
            pltpu.VMEM((L, INNER), F32),
            pltpu.VMEM((L, INNER), F32),
            pltpu.VMEM((L, INNER), F32),
            pltpu.VMEM((L, INNER), F32),
            pltpu.VMEM((L, N), F32),
            pltpu.VMEM((L, N), F32),
            pltpu.VMEM((8, L), F32),
            pltpu.VMEM((16 + L, CH), F32),
            pltpu.VMEM((NO, 2 * RC, INNER), F32),
            pltpu.VMEM((NO, 1, INNER), F32),
            pltpu.VMEM((NO, RC, INNER), F32),
            pltpu.VMEM((NO, RC, INNER), F32),
            pltpu.VMEM((2, NX, RC, INNER), F32),
            pltpu.VMEM((NX, 1, INNER), F32),
            pltpu.VMEM((2, NX, 2 * RC, INNER), F32),
            pltpu.VMEM((2, NX, 2 * RC, INNER), F32),
            pltpu.VMEM((2, 8, INNER), F32),
            pltpu.VMEM((2, 8, INNER), F32),
            pltpu.VMEM((NX, 8, CH + 2 * INNER), F32),
            pltpu.VMEM((NX, 16, CH), F32),
            pltpu.VMEM((N, INNER), F32),
            pltpu.VMEM((2, NX, RC, INNER), F32),
            pltpu.VMEM((NO, 2 * RC, INNER), F32),
            pltpu.VMEM((NO, 2 * RC, INNER), F32),
            pltpu.VMEM((8, CH), F32),
            pltpu.VMEM((8, CH), F32),
            pltpu.VMEM((8, CH), F32),
            pltpu.VMEM((8, CH), F32),
            pltpu.VMEM((NR, 1, 128), F32),
            pltpu.VMEM((NR, 1, 128), F32),
            pltpu.VMEM((ZR, 1, 128), F32),
            pltpu.VMEM((2, 1, 128), F32),
            pltpu.VMEM((NR, 1, 128), F32),
            pltpu.SemaphoreType.DMA((2, NX)),
            pltpu.SemaphoreType.DMA((2, NX)),
            pltpu.SemaphoreType.DMA((2,)),
            pltpu.SemaphoreType.DMA((2,)),
            pltpu.SemaphoreType.DMA((3,)),
            pltpu.SemaphoreType.DMA((3,)),
            pltpu.SemaphoreType.DMA((2, NX)),
            pltpu.SemaphoreType.DMA((2, NX)),
            pltpu.SemaphoreType.DMA((NO,)),
            pltpu.SemaphoreType.DMA((1,)),
            pltpu.SemaphoreType.DMA((1,)),
            pltpu.SemaphoreType.DMA((1,)),
            pltpu.SemaphoreType.DMA((1,)),
            pltpu.SemaphoreType.DMA((3,)),
            pltpu.SemaphoreType.DMA((3,)),
            pltpu.SemaphoreType.REGULAR,
            pltpu.SemaphoreType.REGULAR,
        ],
        compiler_params=pltpu.CompilerParams(
            collective_id=0, has_side_effects=True, vmem_limit_bytes=48 << 20
        ),
        name="slab",
    )(dt_bias, a_log, d_skip, raw, weight, bias, dt_t, cot)


def on_device(xbc_raw, conv_weight, conv_bias, dt_raw, dt_bias, a_log, d_skip, grad_out):
    raw = xbc_raw[0]
    gx, gpre, weight_grad, bias_grad, small = run_main(
        raw, conv_weight, conv_bias[None], dt_raw[0].T, dt_bias, a_log, d_skip, grad_out[0]
    )
    return (
        gx[None], gpre.T[None], weight_grad, bias_grad[0], small[0, 0:4], small[0, 8:12],
        small[0, 16:20],
    )


def solution(mesh):
    rows = P("dp", "ctx", None)
    return jax.shard_map(
        on_device,
        mesh=mesh,
        in_specs=(rows, P(), P(), rows, P(), P(), P(), rows),
        out_specs=(rows, rows, P(), P(), P(), P(), P()),
        check_vma=False,
    )
```

time: 130 us -> 96.9 us (0.75)
  Pallas kernels: 118 us -> 89.7 us
  starting transfers between devices: 4.49 us -> 0 us
    pallas_call x1, Pallas kernels: 118 us -> 89.7 us  [run_main(): pl.pallas_call(main_kernel, out_shape=(jax.ShapeDtypeStruct((L, CH), BF16...]
    ppermute x1 -> x0, starting transfers between devices: 4.49 us -> none  [shift(): return lax.ppermute(block, axis, route)]
  transfers between devices with their start and end apart: 1 -> 0, of which waited for: 1 -> 0; matrix products, arithmetic and copies ran while one was open for 0% -> 0% of each run, Pallas kernels for 0% -> 0%
where the time goes in v3:
time: 96.9 us; the launch traced here: 96.7 us
  Pallas kernels  89.7 us (93%)
  local copies, waits for them, and re-layouts  6.29 us (6%)
    pallas_call x1, Pallas kernels, run_main(): pl.pallas_call(main_kernel, out_shape=(jax.ShapeDtypeStruct((L, CH), BF16...  89.7 us
    unnamed x20, local copies, waits for them, and re-layouts  5.7 us

profile of v3, /device:TPU:1, one launch (start us, length us, event | category | flops | bytes accessed | tf_op | source)
XLA Modules:
  0.0 96.7 jit_solution(1444398693803005998)
XLA Ops:
  0.6 0.0 copy-start.3
  0.6 0.0 copy-start.4
  0.7 0.0 copy-start.5
  0.7 0.0 copy-start.6
  0.7 0.0 copy-start.7
  0.7 0.6 copy-done.3
  1.3 0.0 copy-done.4
  1.3 0.0 copy-done.5
  1.3 0.0 copy-done.6
  1.3 0.0 copy-done.7
  1.4 0.0 copy-start
  1.4 0.9 copy-done
  2.3 0.0 copy-start.1
  2.3 0.9 copy-done.1
  3.2 0.0 copy-start.2
  3.2 0.7 copy-done.2
  3.9 89.7 %slab.1 = (bf16[256,512]{1,0:T(8,128)(2,1)S(1)}, f32[4,256]{1,0:T(4,128)S(1)}, f32[4,512]{1,0:T(4,128)S(1)}, f32[1,512]{1,0:T(1,128)S(1)}, f32[1,128]{1,0:T(1,128)S(1)}) custom-call(f32[4]{0:T(128)S(1)} %copy-done.5, f32[4]{0:T(128)S(1)} %copy-done.6, f32[4]{0:T(128)S(1)} %copy-done.7, bf16[256,512]{1,0:T(8,128)(2,1)S(1)} %bitcast.17, ...), custom_call_target="tpu_custom_call" | custom-call | tf_op jit(solution)/shard_map/slab/pallas_call | solution.py:734
  93.6 0.6 slice_bitcast_fusion
  94.2 0.7 copy.19
  94.9 0.6 copy.20
  95.5 0.6 copy.21
  96.1 0.6 copy.22
Async XLA Ops:
  0.6 0.7 copy-start.3
  0.6 0.7 copy-start.4
  0.7 0.7 copy-start.5
  0.7 0.7 copy-start.6
  0.7 0.7 copy-start.7
  1.4 0.9 copy-start
  2.3 0.9 copy-start.1
  3.2 0.7 copy-start.2

commit v4 on v3

--- a/solution.py
+++ b/solution.py
@@ -85,9 +85,9 @@
 
 
 def main_kernel(
-    dt_bias_ref, a_log_ref, skip_ref, raw_hbm, w_hbm, bias_hbm, dt_hbm, cot_hbm,
+    dt_bias_hbm, a_log_hbm, skip_hbm, raw_hbm, w_hbm, bias_hbm, dt_hbm, cot_hbm,
     gx_ref, gpre_ref, wg_ref, bg_ref, small_ref,
-    raw_ref, w_ref, bias_ref, dt_ref, cot_ref, in_sem,
+    dt_bias_ref, a_log_ref, skip_ref, raw_ref, w_ref, bias_ref, dt_ref, cot_ref, in_sem,
     xp, pre_s, sig_s, xb, rows_s, cols_s, loc, dec, tw_e, up_e, st_e, ac, gbl, gcl, pair_s,
     gc_pad, abuf, dbuf, pre_p, pre_q, tot, blk, rbuf, sbuf, rfac, sfac, heads, tails, cfull, corr,
     rsend, ret, near_out, near_in, spill_out, spill_in, sums_ref, plane, line, own, totals,
@@ -128,7 +128,8 @@
         pltpu.make_async_copy(src, dst, in_sem.at[i])
         for i, (src, dst) in enumerate(
             ((raw_hbm, raw_ref), (w_hbm, w_ref), (bias_hbm, bias_ref), (dt_hbm, dt_ref),
-             (cot_hbm, cot_ref))
+             (cot_hbm, cot_ref), (dt_bias_hbm, dt_bias_ref), (a_log_hbm, a_log_ref),
+             (skip_hbm, skip_ref))
         )
     ]
     for copy in inputs:
@@ -327,19 +328,19 @@
             else:
                 gcl[t0:, :] += from_here
 
-    @pl.when(z > 0)
-    def _():
-        local_terms()
-
     left = zq < NB // 2
 
     @pl.when(left)
     def _():
         relay_heads()
 
-    @pl.when(jnp.logical_not(left))
+    @pl.when(zq > 0)
     def _():
         relay_tails()
+
+    @pl.when(zq == NB // 2)
+    def _():
+        relay_heads()
 
     from_block(dbuf, 0).wait_recv()
     from_block(abuf, 1).wait_recv()
@@ -424,18 +425,18 @@
     @pl.when(left)
     def _():
         relay(0)
+
+    @pl.when(jnp.logical_not(left))
+    def _():
+        relay(1)
+
+    @pl.when(zq == 0)
+    def _():
         relay_tails()
 
-    @pl.when(jnp.logical_not(left))
-    def _():
-        relay(1)
+    @pl.when(zq == NB - 1)
+    def _():
         relay_heads()
-
-    @pl.when(z == 0)
-    def _():
-        xp[5:8, :] = tails[x, 0:3, :]
-        activate(0, 16)
-        local_terms()
 
     mine_rows = pl.ds(pl.multiple_of(me_o * RC, RC), RC)
     for l in range(NX):
@@ -504,6 +505,13 @@
 
     lax.fori_loop(1, NO, back, 0)
     ret[pl.ds(me_o, 1)] = rsend[pl.ds(me_o, 1)]
+
+    @pl.when(z == 0)
+    def _():
+        xp[5:8, :] = tails[x, 0:3, :]
+        activate(0, 16)
+
+    local_terms()
 
     @pl.when(zq == 0)
     def _():
@@ -729,8 +737,7 @@
 
 def run_main(raw, weight, bias, dt_t, dt_bias, a_log, d_skip, cot):
     vmem = pl.BlockSpec(memory_space=pltpu.VMEM)
-    smem = pl.BlockSpec(memory_space=pltpu.SMEM)
-    hbm = pl.BlockSpec(memory_space=pl.ANY)
+    hbm = pl.BlockSpec(memory_space=pltpu.HBM)
     return pl.pallas_call(
         main_kernel,
         out_shape=(
@@ -740,15 +747,18 @@
             jax.ShapeDtypeStruct((1, CH), F32),
             jax.ShapeDtypeStruct((1, 128), F32),
         ),
-        in_specs=[smem] * 3 + [hbm] * 5,
+        in_specs=[hbm] * 8,
         out_specs=(vmem,) * 5,
         scratch_shapes=[
+            pltpu.SMEM((H,), F32),
+            pltpu.SMEM((H,), F32),
+            pltpu.SMEM((H,), F32),
             pltpu.VMEM((L, CH), BF16),
             pltpu.VMEM((K, CH), F32),
             pltpu.VMEM((1, CH), F32),
             pltpu.VMEM((H, L), F32),
             pltpu.VMEM((L, INNER), BF16),
-            pltpu.SemaphoreType.DMA((5,)),
+            pltpu.SemaphoreType.DMA((8,)),
             pltpu.VMEM((8 + L, CH), F32),
             pltpu.VMEM((L, CH), F32),
             pltpu.VMEM((L, CH), F32),
@@ -809,20 +819,41 @@
             pltpu.SemaphoreType.REGULAR,
         ],
         compiler_params=pltpu.CompilerParams(
-            collective_id=0, has_side_effects=True, vmem_limit_bytes=48 << 20
+            collective_id=0, has_side_effects=True, vmem_limit_bytes=67043328
         ),
         name="slab",
     )(dt_bias, a_log, d_skip, raw, weight, bias, dt_t, cot)
 
 
+def finish_kernel(gx, gpre, wg, bg, small, gx_o, gpre_o, wg_o, bg_o, db_o, da_o, ds_o):
+    gx_o[...] = gx[...]
+    gpre_o[...] = gpre[...]
+    wg_o[...] = wg[...]
+    bg_o[...] = bg[...]
+    db_o[...] = small[0:1, 0:4]
+    da_o[...] = small[0:1, 8:12]
+    ds_o[...] = small[0:1, 16:20]
+
+
+def finish(*parts):
+    vmem = pl.BlockSpec(memory_space=pltpu.VMEM)
+    head = jax.ShapeDtypeStruct((1, H), F32)
+    return pl.pallas_call(
+        finish_kernel,
+        out_shape=tuple(jax.ShapeDtypeStruct(p.shape, p.dtype) for p in parts[:4]) + (head,) * 3,
+        in_specs=[vmem] * 5,
+        out_specs=(vmem,) * 7,
+        compiler_params=pltpu.CompilerParams(vmem_limit_bytes=67043328),
+        name="finish",
+    )(*parts)
+
+
 def on_device(xbc_raw, conv_weight, conv_bias, dt_raw, dt_bias, a_log, d_skip, grad_out):
-    raw = xbc_raw[0]
-    gx, gpre, weight_grad, bias_grad, small = run_main(
-        raw, conv_weight, conv_bias[None], dt_raw[0].T, dt_bias, a_log, d_skip, grad_out[0]
-    )
+    gx, gpre, weight_grad, bias_grad, bias, decay, skip = finish(*run_main(
+        xbc_raw[0], conv_weight, conv_bias[None], dt_raw[0].T, dt_bias, a_log, d_skip, grad_out[0]
+    ))
     return (
-        gx[None], gpre.T[None], weight_grad, bias_grad[0], small[0, 0:4], small[0, 8:12],
-        small[0, 16:20],
+        gx[None], gpre.T[None], weight_grad, bias_grad[0], bias[0], decay[0], skip[0],
     )
 
 

time: 96.9 us -> 91.7 us (0.946)
  local copies, waits for them, and re-layouts: 6.29 us -> 0 us
  Pallas kernels: 89.7 us -> 90.9 us
    unnamed x20 -> x0, local copies, waits for them, and re-layouts: 5.7 us -> none
    pallas_call x0 -> x1, Pallas kernels: none -> 1.69 us  [finish(): pl.pallas_call(finish_kernel, out_shape=tuple((jax.ShapeDtypeStruct(p.sha...]
where the time goes in v4:
time: 91.7 us; the launch traced here: 91.5 us
  Pallas kernels  90.9 us (99%)
    pallas_call x1, Pallas kernels, run_main(): pl.pallas_call(main_kernel, out_shape=(jax.ShapeDtypeStruct((L, CH), BF16...  89.2 us

profile of v4, /device:TPU:1, one launch (start us, length us, event | category | flops | bytes accessed | tf_op | source)
XLA Modules:
  0.0 91.5 jit_solution(5203142455428280572)
XLA Ops:
  0.6 89.2 %slab.1 = (bf16[256,512]{1,0:T(8,128)(2,1)}, f32[4,256]{1,0:T(4,128)}, f32[4,512]{1,0:T(4,128)}, f32[1,512]{1,0:T(1,128)}, f32[1,128]{1,0:T(1,128)}) custom-call(f32[4]{0:T(128)} %dt_bias_hbm.1, f32[4]{0:T(128)} %a_log_hbm.1, f32[4]{0:T(128)} %skip_hbm.1, bf16[256,512]{1,0:T(8,128)(2,1)} %bitcast.14, f32[4,512]{1,0:T(4,128)} %w_hbm.1, f32[1,512]{1,0:T(1,128)} %bitcast.17, ...), custom_call_target="tpu_custom_call" | custom-call | tf_op jit(solution)/shard_map/slab/pallas_call | solution.py:741
  89.8 1.7 %finish.1 = (bf16[256,512]{1,0:T(8,128)(2,1)}, f32[4,256]{1,0:T(4,128)}, f32[4,512]{1,0:T(4,128)}, f32[1,512]{1,0:T(1,128)}, f32[1,4]{1,0:T(1,128)}, /*index=5*/f32[1,4]{1,0:T(1,128)}, f32[1,4]{1,0:T(1,128)}) custom-call(bf16[256,512]{1,0:T(8,128)(2,1)} %get-tuple-element.19.gx, f32[4,256]{1,0:T(4,128)} %get-tuple-element.20.gpre, ...), custom_call_target="tpu_custom_call" | custom-call | tf_op jit(solution)/shard_map/finish/pallas_call | solution.py:841

commit v5 on v4

--- a/solution.py
+++ b/solution.py
@@ -370,8 +370,9 @@
     first = jnp.where(left, 0, 1)
 
     def hop(way, l):
+        rows = slice(0, RC if l == (0, NX - 1)[way] else 2 * RC)
         return remote(
-            sbuf.at[way, l], rbuf.at[way, l], send_sem.at[way, l], recv_sem.at[way, l],
+            sbuf.at[way, l, rows], rbuf.at[way, l, rows], send_sem.at[way, l], recv_sem.at[way, l],
             along_line(1 - 2 * way),
         )
 
@@ -417,9 +418,10 @@
             @pl.when(has_out(way))
             def _():
                 sbuf[way, l, 0:RC, :] = blk[l] * rbuf[way, l, 0:RC, :] + tot[way, l]
-                sbuf[way, l, RC:, :] = (
-                    rbuf[way, l, RC:, :] + rfac[way, l : l + 1, :] * tot[1 - way, l]
-                )
+                if l != (0, NX - 1)[way]:
+                    sbuf[way, l, RC:, :] = (
+                        rbuf[way, l, RC:, :] + rfac[way, l : l + 1, :] * tot[1 - way, l]
+                    )
                 hop(way, l).start()
 
     @pl.when(left)
@@ -478,6 +480,8 @@
                 here = here + pre_p[NB * l + i]
             give_back(l, i, here, 0)
             at = at * dbuf[NB * l + i]
+        if l == NX - 1:
+            break
         total = (
             e * (blk[l] * rbuf[0, l, 0:RC, :] + tot[0, l] + weights[4] * corr[0, l])
             + rbuf[1, l, RC:, :]
@@ -493,6 +497,8 @@
                 here = here + pre_q[NB * l + i]
             give_back(l, i, here, 1)
             at = at * dbuf[NB * l + i]
+        if l == 0:
+            break
         total = (
             f * (blk[l] * rbuf[1, l, 0:RC, :] + tot[1, l]) + rbuf[0, l, RC:, :] + corr[1, l]
         )

time: 91.7 us -> 90.6 us (0.988)
  Pallas kernels: 90.9 us -> 89.8 us
    pallas_call x1, Pallas kernels: 89.2 us -> 88.1 us  [run_main(): pl.pallas_call(main_kernel, out_shape=(jax.ShapeDtypeStruct((L, CH), BF16...]
where the time goes in v5:
time: 90.6 us; the launch traced here: 90.4 us
  Pallas kernels  89.8 us (99%)
    pallas_call x1, Pallas kernels, run_main(): pl.pallas_call(main_kernel, out_shape=(jax.ShapeDtypeStruct((L, CH), BF16...  88.1 us

profile of v5, /device:TPU:1, one launch (start us, length us, event | category | flops | bytes accessed | tf_op | source)
XLA Modules:
  0.0 90.4 jit_solution(13493582563311926186)
XLA Ops:
  0.6 88.1 %slab.1 = (bf16[256,512]{1,0:T(8,128)(2,1)}, f32[4,256]{1,0:T(4,128)}, f32[4,512]{1,0:T(4,128)}, f32[1,512]{1,0:T(1,128)}, f32[1,128]{1,0:T(1,128)}) custom-call(f32[4]{0:T(128)} %dt_bias_hbm.1, f32[4]{0:T(128)} %a_log_hbm.1, f32[4]{0:T(128)} %skip_hbm.1, bf16[256,512]{1,0:T(8,128)(2,1)} %bitcast.14, f32[4,512]{1,0:T(4,128)} %w_hbm.1, f32[1,512]{1,0:T(1,128)} %bitcast.17, ...), custom_call_target="tpu_custom_call" | custom-call | tf_op jit(solution)/shard_map/slab/pallas_call | solution.py:747
  88.7 1.7 %finish.1 = (bf16[256,512]{1,0:T(8,128)(2,1)}, f32[4,256]{1,0:T(4,128)}, f32[4,512]{1,0:T(4,128)}, f32[1,512]{1,0:T(1,128)}, f32[1,4]{1,0:T(1,128)}, /*index=5*/f32[1,4]{1,0:T(1,128)}, f32[1,4]{1,0:T(1,128)}) custom-call(bf16[256,512]{1,0:T(8,128)(2,1)} %get-tuple-element.19.gx, f32[4,256]{1,0:T(4,128)} %get-tuple-element.20.gpre, ...), custom_call_target="tpu_custom_call" | custom-call | tf_op jit(solution)/shard_map/finish/pallas_call | solution.py:847

commit v6 on v5

--- a/solution.py
+++ b/solution.py
@@ -132,8 +132,6 @@
              (skip_hbm, skip_ref))
         )
     ]
-    for copy in inputs:
-        copy.start()
     for step in (1, ZR - 1, NB, ZR - NB):
         pl.semaphore_signal(
             barrier, inc=1, device_id=device(x, y, lax.rem(ring + step, ZR), core),
@@ -150,6 +148,8 @@
         pl.semaphore_signal(
             barrier, inc=1, device_id=device(x, q // 2, ring, lax.rem(q, 2)), device_id_type=MESH
         )
+    for copy in inputs:
+        copy.start()
     for copy in inputs:
         copy.wait()
 
@@ -537,6 +537,16 @@
         pl.semaphore_wait(edge_sem, 1)
         pl.semaphore_signal(known_sem, inc=1, device_id=along_line(-1), device_id_type=MESH)
 
+    cot = cot_ref[...].astype(F32)
+    vals = xb[:, :INNER].astype(F32)
+    local_step = head_sums(vals * ac[...])
+    sel = head_rows(F32)
+    skip_sum = jnp.sum(sel * jnp.sum(cot * vals, axis=0, keepdims=True), axis=1, keepdims=True)
+    skip_lanes = spread(jnp.broadcast_to(0.0, (8, 128)) + sum(
+        jnp.where(iota((8, 128), 1) == h, skip_ref[h], 0.0) for h in range(H)
+    ), 0)[0:1, :]
+    ac[...] = st_e[...] * ac[...] + skip_lanes * cot
+
     from_block(ret, 2).wait_recv()
     s_in = ret[:, 0:RC, :].reshape(N, INNER)
     g_after = ret[:, RC:, :].reshape(N, INNER)
@@ -547,27 +557,19 @@
     g_hi, g_lo = split(g_after)
     state_back = dot(b_val, g_hi) + dot(b_val, g_lo)
     state_proj = dot(c_val, s_hi) + dot(c_val, s_lo)
-    cot = cot_ref[...].astype(F32)
-    vals = xb[:, :INNER].astype(F32)
     scaled = cot * up_e[...]
     hi, lo = split(scaled)
     grad_c = gcl[...] + dot_nt(hi, s_hi) + dot_nt(hi, s_lo) + dot_nt(lo, s_hi)
     hi, lo = split(vals * tw_e[...])
     grad_b = gbl[...] + dot_nt(hi, g_hi) + dot_nt(hi, g_lo) + dot_nt(lo, g_hi)
-    local_step = head_sums(vals * ac[...])
     tail_grad = head_sums(vals * state_back)
     proj_term = head_sums(scaled * state_proj)
-    skip_lanes = spread(jnp.broadcast_to(0.0, (8, 128)) + sum(
-        jnp.where(iota((8, 128), 1) == h, skip_ref[h], 0.0) for h in range(H)
-    ), 0)[0:1, :]
-    grad_vals = st_e[...] * ac[...] + skip_lanes * cot + tw_e[...] * state_back
+    grad_vals = ac[...] + tw_e[...] * state_back
 
     step = rows_s[8:16, :]
     tw = rows_s[16:24, :]
     cum = rows_s[0:8, :]
     cum_last = cum[:, L - 1 : L]
-    sel = head_rows(F32)
-    skip_sum = jnp.sum(sel * jnp.sum(cot * vals, axis=0, keepdims=True), axis=1, keepdims=True)
     both = jnp.sum(
         sel * jnp.sum(s_in * g_after, axis=0, keepdims=True), axis=1, keepdims=True
     )

time: 90.6 us -> 90.7 us (level)
  no operation moved by 1% of the time
where the time goes in v6:
time: 90.7 us; the launch traced here: 90.5 us
  Pallas kernels  89.8 us (99%)
    pallas_call x1, Pallas kernels, run_main(): pl.pallas_call(main_kernel, out_shape=(jax.ShapeDtypeStruct((L, CH), BF16...  88.2 us

profile of v6, /device:TPU:1, one launch (start us, length us, event | category | flops | bytes accessed | tf_op | source)
XLA Modules:
  0.0 90.5 jit_solution(12141534941336136690)
XLA Ops:
  0.6 88.2 %slab.1 = (bf16[256,512]{1,0:T(8,128)(2,1)}, f32[4,256]{1,0:T(4,128)}, f32[4,512]{1,0:T(4,128)}, f32[1,512]{1,0:T(1,128)}, f32[1,128]{1,0:T(1,128)}) custom-call(f32[4]{0:T(128)} %dt_bias_hbm.1, f32[4]{0:T(128)} %a_log_hbm.1, f32[4]{0:T(128)} %skip_hbm.1, bf16[256,512]{1,0:T(8,128)(2,1)} %bitcast.14, f32[4,512]{1,0:T(4,128)} %w_hbm.1, f32[1,512]{1,0:T(1,128)} %bitcast.17, ...), custom_call_target="tpu_custom_call" | custom-call | tf_op jit(solution)/shard_map/slab/pallas_call | solution.py:749
  88.8 1.7 %finish.1 = (bf16[256,512]{1,0:T(8,128)(2,1)}, f32[4,256]{1,0:T(4,128)}, f32[4,512]{1,0:T(4,128)}, f32[1,512]{1,0:T(1,128)}, f32[1,4]{1,0:T(1,128)}, /*index=5*/f32[1,4]{1,0:T(1,128)}, f32[1,4]{1,0:T(1,128)}) custom-call(bf16[256,512]{1,0:T(8,128)(2,1)} %get-tuple-element.19.gx, f32[4,256]{1,0:T(4,128)} %get-tuple-element.20.gpre, ...), custom_call_target="tpu_custom_call" | custom-call | tf_op jit(solution)/shard_map/finish/pallas_call | solution.py:849
